TPU v7x, 512 devices: a whole 4x4x16 slice. The times are simulated.
512 devices in a mesh: wide: 64 (over z, x), narrow: 8 (over y, core).
Axes of the slice: x: 4, y: 4, z: 16, core: 2. Of those that a mesh axis runs over, the one named last changes fastest.
Arguments:
- sublevel_symbol_entries: bfloat16 [1024, 4, 4096], P('wide', None, 'narrow'), may hold values from -160 to 160
- prior_symbol_memory: bfloat16 [1024, 4096], P('wide', 'narrow'), may hold values from -6 to 6
- entry_scaling_multiplier: float32 [4096], P('narrow'), may hold values from 0.25 to 1.75
- entry_scaling_offset: float32 [4096], P('narrow'), may hold values from -4 to 4
- learned_blending: float32 [6, 4096], P(None, 'narrow'), may hold values from 0 to 1
- blending_lowering_coefficients: bfloat16 [4096, 160], P('narrow'), may hold values from -0.09375 to 0.09375
- blending_raising_coefficients: bfloat16 [5, 32, 4096], P(None, None, 'narrow'), may hold values from -1 to 1
- fading_lowering_coefficients: bfloat16 [4096, 64], P('narrow'), may hold values from -0.09375 to 0.09375
- fading_raising_coefficients: bfloat16 [64, 4096], P(None, 'wide'), may hold values from -0.75 to 0.75
- learned_fading: float32 [4096], P('wide'), may hold values from -6 to 1
- immediate_item_premium: float32 [4096], P('wide'), may hold values from -3 to 3
- acceptor_projection: bfloat16 [4096, 4096], P('narrow', 'wide'), may hold values from -0.09375 to 0.09375
- lookup_projection: bfloat16 [4096, 4096], P('narrow', 'wide'), may hold values from -0.09375 to 0.09375
- payload_projection: bfloat16 [4096, 4096], P('narrow', 'wide'), may hold values from -0.09375 to 0.09375
- gating_projection: bfloat16 [4096, 4096], P('narrow', 'wide'), may hold values from -0.09375 to 0.09375
- emission_projection: bfloat16 [4096, 4096], P(None, 'wide'), may hold values from -0.09375 to 0.09375
- group_scaling_multiplier: float32 [4096], P('wide'), may hold values from 0.25 to 1.75
- group_scaling_offset: float32 [4096], P('wide'), may hold values from -4 to 4
- dialogue_group_memory: float32 [262144, 1024], P('wide', 'narrow'), may hold values from -6 to 6
Outputs:
- mixing_output: bfloat16 [1024, 4, 4096], P('narrow', None, 'wide')
- final_state: float32 [262144, 1024], P('wide', 'narrow')
All inputs are finite; a program needn't handle non-finite values.
Results may differ from a plain program's by a relative error of at most 0.034.
Values may be sent and summed in bfloat16 or wider, within the bound.
A program may use at most 64 MiB of HBM per device.

v0:
```python
import jax
import jax.numpy as jnp
from jax import lax
from jax.sharding import PartitionSpec as P

CHANNEL_SPAN = 64
FEATURE_EXTENT = 4096


def per_device(
    sublevel_symbol_entries,
    prior_symbol_memory,
    entry_scaling_multiplier,
    entry_scaling_offset,
    learned_blending,
    blending_lowering_coefficients,
    blending_raising_coefficients,
    fading_lowering_coefficients,
    fading_raising_coefficients,
    learned_fading,
    immediate_item_premium,
    acceptor_projection,
    lookup_projection,
    payload_projection,
    gating_projection,
    emission_projection,
    group_scaling_multiplier,
    group_scaling_offset,
    dialogue_group_memory,
):
    rank = blending_raising_coefficients.shape[1]
    narrow_rows = dialogue_group_memory.shape[1]
    local_width = emission_projection.shape[1]
    group_partition = local_width // CHANNEL_SPAN
    weights = (acceptor_projection, lookup_projection, payload_projection, gating_projection)
    shift_gathered = lax.all_gather(prior_symbol_memory, "wide", axis=0, tiled=True)

    def channel_set_first(block):
        return block.reshape(narrow_rows, group_partition, CHANNEL_SPAN).transpose(1, 2, 0)

    present_symbol = dialogue_group_memory.reshape(
        group_partition, CHANNEL_SPAN, CHANNEL_SPAN, narrow_rows
    )
    previous_rows = prior_symbol_memory
    previous_all = shift_gathered
    results = []
    for index in range(sublevel_symbol_entries.shape[1]):
        floats = sublevel_symbol_entries[:, index : index + 1].astype(jnp.float32)
        totals, squares = lax.psum((jnp.sum(floats, -1), jnp.sum(floats * floats, -1)), "narrow")
        prepare_center = totals[..., None] / FEATURE_EXTENT
        spread = squares[..., None] / FEATURE_EXTENT - prepare_center * prepare_center
        normed = (
            (floats - prepare_center) * lax.rsqrt(spread + 1e-05) * entry_scaling_multiplier
            + entry_scaling_offset
        ).astype(jnp.bfloat16)
        previous = jnp.concatenate([previous_rows[:, None], normed[:, :-1]], 1)
        prepare_normalized_float = normed.astype(jnp.float32)
        prepare_shifted_input = previous.astype(jnp.float32) - prepare_normalized_float
        blended = (prepare_normalized_float + prepare_shifted_input * learned_blending[0]).astype(
            jnp.bfloat16
        )
        partial_mix = jnp.einsum(
            "smd,dr->smr",
            blended,
            blending_lowering_coefficients,
            preferred_element_type=jnp.float32,
        )
        hidden_activation = jnp.tanh(lax.psum(partial_mix, "narrow")).astype(jnp.bfloat16)
        decay_shift = jnp.einsum(
            "smr,rd->smd",
            hidden_activation[..., :rank],
            blending_raising_coefficients[0],
            preferred_element_type=jnp.float32,
        )
        decay_mix = (
            prepare_normalized_float + prepare_shifted_input * (learned_blending[1] + decay_shift)
        ).astype(jnp.bfloat16)
        partial_decay = jnp.einsum(
            "smd,dr->smr",
            decay_mix,
            fading_lowering_coefficients,
            preferred_element_type=jnp.float32,
        )
        decay_hidden = jnp.tanh(lax.psum(partial_decay, "narrow")).astype(jnp.bfloat16)
        small = jnp.concatenate([hidden_activation[..., rank:], decay_hidden], -1)
        prepare_normed_all = lax.all_gather(normed, "wide", axis=0, tiled=True)
        prepare_small_all = lax.all_gather(small, "wide", axis=0, tiled=True)
        normed, normed_all, small_all = (normed, prepare_normed_all, prepare_small_all)
        project_previous_all = previous_all[:, None]
        normalized_float = normed_all.astype(jnp.float32)
        shifted_input = project_previous_all.astype(jnp.float32) - normalized_float
        term_results = []
        for selector_index in range(4):
            low_rank_update = jnp.einsum(
                "smr,rd->smd",
                small_all[..., selector_index * rank : (selector_index + 1) * rank],
                blending_raising_coefficients[selector_index + 1],
                preferred_element_type=jnp.float32,
            )
            mixed_input = (
                normalized_float
                + shifted_input * (learned_blending[selector_index + 2] + low_rank_update)
            ).astype(jnp.bfloat16)
            term_results.append(
                jnp.einsum(
                    "smd,de->sme",
                    mixed_input,
                    weights[selector_index],
                    preferred_element_type=jnp.float32,
                )
            )
        project_transformed_outcome = lax.psum_scatter(
            jnp.concatenate(term_results, -1).astype(jnp.bfloat16),
            "narrow",
            scatter_dimension=0,
            tiled=True,
        ).astype(jnp.float32)
        rows_start = lax.axis_index("narrow") * narrow_rows
        decay_rows = lax.dynamic_slice_in_dim(
            small_all[..., 4 * rank :], rows_start, narrow_rows, 0
        )
        decay_log = learned_fading + jnp.einsum(
            "smr,rd->smd",
            decay_rows,
            fading_raising_coefficients,
            preferred_element_type=jnp.float32,
        )
        shrink_coefficient = jnp.exp(-jnp.exp(decay_log))
        recurrence_present_symbol = present_symbol
        each_group_reward = immediate_item_premium.reshape(group_partition, CHANNEL_SPAN)
        present_acceptor = channel_set_first(project_transformed_outcome[:, 0, :local_width])
        key_now = channel_set_first(
            project_transformed_outcome[:, 0, local_width : 2 * local_width]
        )
        value_now = channel_set_first(
            project_transformed_outcome[:, 0, 2 * local_width : 3 * local_width]
        )
        gate_now = project_transformed_outcome[:, 0, 3 * local_width :]
        forget_now = channel_set_first(shrink_coefficient[:, 0])
        dyadic_tensor = key_now[:, :, None, :] * value_now[:, None, :, :]
        memory_retrieval = jnp.sum(
            present_acceptor[:, :, None, :]
            * (recurrence_present_symbol + each_group_reward[:, :, None, None] * dyadic_tensor),
            1,
        )
        recurrence_present_symbol = (
            forget_now[:, :, None, :] * recurrence_present_symbol + dyadic_tensor
        )
        center = jnp.mean(memory_retrieval, 1, keepdims=True)
        offset = memory_retrieval - center
        scaled = offset * lax.rsqrt(jnp.mean(offset * offset, 1, keepdims=True) + 0.00064)
        squashed_vector = scaled.transpose(2, 0, 1).reshape(narrow_rows, local_width)
        pieces = [
            (
                (squashed_vector * group_scaling_multiplier + group_scaling_offset)
                * jax.nn.silu(gate_now)
            ).astype(jnp.bfloat16)
        ]
        present_symbol = recurrence_present_symbol
        gated = jnp.stack(pieces, 1)
        results.append(
            jnp.einsum(
                "smc,ce->sme",
                lax.all_gather(gated, "wide", axis=2, tiled=True),
                emission_projection,
                preferred_element_type=jnp.float32,
            ).astype(jnp.bfloat16)
        )
        previous_rows = normed[:, 0]
        previous_all = normed_all[:, 0]
    mixing_output = jnp.concatenate(results, 1)
    return (
        mixing_output,
        present_symbol.reshape(group_partition * CHANNEL_SPAN * CHANNEL_SPAN, narrow_rows),
    )


def solution(mesh):
    placed = (
        P("wide", None, "narrow"),
        P("wide", "narrow"),
        P("narrow"),
        P("narrow"),
        P(None, "narrow"),
        P("narrow", None),
        P(None, None, "narrow"),
        P("narrow", None),
        P(None, "wide"),
        P("wide"),
        P("wide"),
        P("narrow", "wide"),
        P("narrow", "wide"),
        P("narrow", "wide"),
        P("narrow", "wide"),
        P(None, "wide"),
        P("wide"),
        P("wide"),
        P("wide", "narrow"),
    )
    return jax.shard_map(
        per_device,
        mesh=mesh,
        in_specs=placed,
        out_specs=(P("narrow", None, "wide"), P("wide", "narrow")),
        check_vma=False,
    )
```

profile of v0, /device:TPU:6, one launch (start us, length us, event | category | flops | bytes accessed | tf_op | source)
XLA Modules:
  0.0 1446.9 jit_solution(15403730953367358589)
XLA Ops:
  7.3 1.1 fusion.287
  8.7 14.9 %all-reduce.2 = (f32[16,1]{0,1:T(1,128)S(1)}, f32[16,1]{0,1:T(1,128)S(1)}, f32[16,1]{0,1:T(1,128)S(1)}, f32[16,1]{0,1:T(1,128)S(1)}, f32[16,1]{0,1:T(1,128)S(1)}...) all-reduce(f32[16,1]{0,1:T(1,128)S(1)} %bitcast.846, ...), channel_id=1, replica_groups=mesh['wide'=64,'narrow'=8] {'narrow'}, use_global_device_ids=true, to_apply=%region_13.14 | all-reduce | flops 128 | bytes 1024 | tf_op jit(solution)/shard_map/psum | solution.py:49
  23.6 1.4 fusion.145
  25.1 0.7 all-gather.20.cloned.1.call-update
  27.8 1.0 fusion.288
  28.7 1.1 convolution_bitcast_fusion
  29.8 1.1 convolution_bitcast_fusion.1
  30.9 1.1 convolution_bitcast_fusion.2
  32.1 1.1 convolution_bitcast_fusion.3
  33.2 24.0 %all-reduce.1 = (f32[16,1,160]{2,0,1:T(8,128)S(1)}, f32[16,1,160]{2,0,1:T(8,128)S(1)}, f32[16,1,160]{2,0,1:T(8,128)S(1)}, f32[16,1,160]{2,0,1:T(8,128)S(1)}) all-reduce(f32[16,1,160]{2,0,1:T(8,128)S(1)} %convolution_bitcast_fusion.1, ...), channel_id=1, replica_groups=mesh['wide'=64,'narrow'=8] {'narrow'}, use_global_device_ids=true, to_apply=%region_24.25 | all-reduce | flops 10240 | bytes 81920 | tf_op jit(solution)/shard_map/psum | solution.py:68
  57.3 1.1 convolution_bitcast_fusion.5
  58.4 1.1 convolution_bitcast_fusion.6
  59.7 1.0 convolution_bitcast_fusion.7
  60.8 1.0 convolution_bitcast_fusion.4
  62.0 24.7 %all-reduce = (f32[16,1,64]{2,0,1:T(8,128)S(1)}, f32[16,1,64]{2,0,1:T(8,128)S(1)}, f32[16,1,64]{2,0,1:T(8,128)S(1)}, f32[16,1,64]{2,0,1:T(8,128)S(1)}) all-reduce(f32[16,1,64]{2,0,1:T(8,128)S(1)} %convolution_bitcast_fusion.5, f32[16,1,64]{2,0,1:T(8,128)S(1)} %convolution_bitcast_fusion.6, ...), channel_id=1, replica_groups=mesh['wide'=64,'narrow'=8] {'narrow'}, use_global_device_ids=true, to_apply=%region_25.26 | all-reduce | flops 4096 | bytes 32768 | tf_op jit(solution)/shard_map/psum | solution.py:84
  86.8 105.9 %all_gather.50 = bf16[1024,1,192]{2,0,1:T(8,128)(2,1)S(1)} all-gather(bf16[16,1,192]{2,0,1:T(8,128)(2,1)S(1)} %pad_maximum_fusion.4), channel_id=1, replica_groups=mesh['wide'=64,'narrow'=8] {'wide'}, dimensions={0}, use_global_device_ids=true | all-gather | bytes 399360 | tf_op jit(solution)/shard_map/all_gather | solution.py:87
  192.7 97.0 %all_gather.41 = bf16[1024,1,192]{2,0,1:T(8,128)(2,1)S(1)} all-gather(bf16[16,1,192]{2,0,1:T(8,128)(2,1)S(1)} %pad_maximum_fusion.1), channel_id=1, replica_groups=mesh['wide'=64,'narrow'=8] {'wide'}, dimensions={0}, use_global_device_ids=true | all-gather | bytes 399360 | tf_op jit(solution)/shard_map/all_gather | solution.py:87
  289.8 99.0 %all_gather.44 = bf16[1024,1,192]{2,0,1:T(8,128)(2,1)S(1)} all-gather(bf16[16,1,192]{2,0,1:T(8,128)(2,1)S(1)} %pad_maximum_fusion.2), channel_id=1, replica_groups=mesh['wide'=64,'narrow'=8] {'wide'}, dimensions={0}, use_global_device_ids=true | all-gather | bytes 399360 | tf_op jit(solution)/shard_map/all_gather | solution.py:87
  388.8 97.0 %all_gather.47 = bf16[1024,1,192]{2,0,1:T(8,128)(2,1)S(1)} all-gather(bf16[16,1,192]{2,0,1:T(8,128)(2,1)S(1)} %pad_maximum_fusion.3), channel_id=1, replica_groups=mesh['wide'=64,'narrow'=8] {'wide'}, dimensions={0}, use_global_device_ids=true | all-gather | bytes 399360 | tf_op jit(solution)/shard_map/all_gather | solution.py:87
  485.7 0.7 slice.308
  487.1 1.0 fusion.83
  488.1 2.4 fusion.75
  490.5 2.4 fusion.74
  493.0 2.4 fusion.73
  495.4 2.3 fusion.72
  497.7 1.0 copy.43
  499.0 79.9 %all-gather.10.cloned.1.call-done = bf16[1024,1,512]{2,0,1:T(8,128)(2,1)} async-done(((bf16[16,1,512]{2,0,1:T(8,128)(2,1)}), bf16[1024,1,512]{2,0,1:T(8,128)(2,1)}) %all-gather.10.cloned.1.call-update) | async-done | bytes 1048592 | tf_op jit(solution)/shard_map/all_gather | solution.py:86
  578.8 2.4 fusion.63
  581.2 2.4 fusion.62
  583.6 2.4 fusion.61
  586.0 2.3 fusion.60
  588.4 1.0 copy.37
  589.4 127.2 %all-gather.16.cloned.1.call-done = bf16[1024,1,512]{2,0,1:T(8,128)(2,1)} async-done(((bf16[16,1,512]{2,0,1:T(8,128)(2,1)}), bf16[1024,1,512]{2,0,1:T(8,128)(2,1)}) %all-gather.16.cloned.1.call-update) | async-done | bytes 1048592 | tf_op jit(solution)/shard_map/all_gather | solution.py:86
  716.7 2.4 fusion.67
  719.1 2.0 fusion.66
  721.2 2.0 fusion.65
  723.2 2.0 fusion.64
  725.2 1.0 copy.39
  726.5 2.0 fusion.71
  728.6 2.1 fusion.70
  730.6 2.1 fusion.69
  732.7 2.0 fusion.68
  734.8 1.0 copy.41
  736.0 19.0 %reduce-scatter.19.cloned.1.call-done = bf16[128,256]{1,0:T(8,128)(2,1)} async-done(((bf16[1024,256]{1,0:T(8,128)(2,1)}), bf16[128,256]{1,0:T(8,128)(2,1)}) %reduce-scatter.19.cloned.1.call-update) | async-done | bytes 65552
  755.1 0.9 copy.44
  756.0 39.6 %reduce-scatter.13.cloned.1.call-done = bf16[128,256]{1,0:T(8,128)(2,1)} async-done(((bf16[1024,256]{1,0:T(8,128)(2,1)}), bf16[128,256]{1,0:T(8,128)(2,1)}) %reduce-scatter.13.cloned.1.call-update) | async-done | bytes 65552
  795.7 0.9 copy.38
  796.6 39.4 %reduce-scatter.15.cloned.1.call-done = bf16[128,256]{1,0:T(8,128)(2,1)} async-done(((bf16[1024,256]{1,0:T(8,128)(2,1)}), bf16[128,256]{1,0:T(8,128)(2,1)}) %reduce-scatter.15.cloned.1.call-update) | async-done | bytes 65552
  836.0 0.9 copy.40
  837.1 40.1 %reduce-scatter.17.cloned.1.call-done = bf16[128,256]{1,0:T(8,128)(2,1)} async-done(((bf16[1024,256]{1,0:T(8,128)(2,1)}), bf16[128,256]{1,0:T(8,128)(2,1)}) %reduce-scatter.17.cloned.1.call-update) | async-done | bytes 65552
  877.2 0.9 copy.42
  879.3 1.1 copy-done.1
  880.3 2.1 fusion.8
  882.4 1.9 fusion.28
  884.3 2.1 fusion.43
  886.6 0.7 fusion.168
  889.4 134.9 %all-gather.14.cloned.1.call-done = bf16[128,1,4096]{0,2,1:T(8,128)(2,1)} async-done(((bf16[128,1,64]{0,2,1:T(8,128)(2,1)}), bf16[128,1,4096]{0,2,1:T(8,128)(2,1)}) %all-gather.14.cloned.1.call-update) | async-done | bytes 1048592 | tf_op jit(solution)/shard_map/all_gather | solution.py:164
  1024.3 1.5 fusion.108
  1025.9 136.4 %all-gather.18.cloned.1.call-done = bf16[128,1,4096]{0,2,1:T(8,128)(2,1)} async-done(((bf16[128,1,64]{0,2,1:T(8,128)(2,1)}), bf16[128,1,4096]{0,2,1:T(8,128)(2,1)}) %all-gather.18.cloned.1.call-update) | async-done | bytes 1048592 | tf_op jit(solution)/shard_map/all_gather | solution.py:164
  1162.3 1.5 fusion.109
  1163.9 136.3 %all-gather.22.cloned.1.call-done = bf16[128,1,4096]{0,2,1:T(8,128)(2,1)} async-done(((bf16[128,1,64]{0,2,1:T(8,128)(2,1)}), bf16[128,1,4096]{0,2,1:T(8,128)(2,1)}) %all-gather.22.cloned.1.call-update) | async-done | bytes 1048592 | tf_op jit(solution)/shard_map/all_gather | solution.py:164
  1300.2 1.5 fusion.110
  1301.7 136.4 %all-gather.26.cloned.1.call-done = bf16[128,1,4096]{0,2,1:T(8,128)(2,1)} async-done(((bf16[128,1,64]{0,2,1:T(8,128)(2,1)}), bf16[128,1,4096]{0,2,1:T(8,128)(2,1)}) %all-gather.26.cloned.1.call-update) | async-done | bytes 1048592 | tf_op jit(solution)/shard_map/all_gather | solution.py:164
  1438.1 1.5 fusion.111
  (130 shorter events, 8.6 us)
Async XLA Ops:
  7.2 1017.2 %copy-start = (bf16[4096,64]{0,1:T(8,128)(2,1)S(1)}, bf16[4096,64]{0,1:T(8,128)(2,1)}, u32[]{:S(2)}) copy-start(bf16[4096,64]{0,1:T(8,128)(2,1)} %param.34) | copy-start | bytes 1572868
  7.2 52.5 %copy-start.4 = (bf16[16,512]{1,0:T(8,128)(2,1)S(1)}, bf16[16,512]{1,0:T(8,128)(2,1)}, u32[]{:S(2)}) copy-start(bf16[16,512]{1,0:T(8,128)(2,1)} %param.20) | copy-start | bytes 49156
  7.2 52.5 %copy-start.2 = (bf16[512,64]{0,1:T(8,128)(2,1)S(1)}, bf16[512,64]{0,1:T(8,128)(2,1)}, u32[]{:S(2)}) copy-start(bf16[512,64]{0,1:T(8,128)(2,1)} %param.26) | copy-start | bytes 196612
  7.2 54.7 %copy-start.7 = (f32[64]{0:T(128)S(1)}, f32[64]{0:T(128)}, u32[]{:S(2)}) copy-start(f32[64]{0:T(128)} %param.29) | copy-start | bytes 772
  7.2 480.9 %all-gather.24.cloned.1.call-start = ((), (), s32[]{:S(2)}) async-start(), calls=%async_computation.11 | async-start | bytes 1064960 | tf_op jit(solution)/shard_map/all_gather | solution.py:86
  25.1 463.0 %all-gather.20.cloned.1.call-start = ((), (), s32[]{:S(2)}) async-start(), calls=%async_computation.9 | async-start | bytes 1064960 | tf_op jit(solution)/shard_map/all_gather | solution.py:86
  25.8 473.1 %all-gather.12.cloned.1.call-start = ((), (), s32[]{:S(2)}) async-start(), calls=%async_computation.5 | async-start | bytes 1064960 | tf_op jit(solution)/shard_map/all_gather | solution.py:36
  26.6 552.3 %all-gather.10.cloned.1.call-start = ((), (), s32[]{:S(2)}) async-start(), calls=%async_computation.4 | async-start | bytes 1064960 | tf_op jit(solution)/shard_map/all_gather | solution.py:86
  27.1 689.5 %all-gather.16.cloned.1.call-start = ((), (), s32[]{:S(2)}) async-start(), calls=%async_computation.7 | async-start | bytes 1064960 | tf_op jit(solution)/shard_map/all_gather | solution.py:86
  27.7 727.3 %reduce-scatter.19.cloned.1.call-start = ((), (), s32[]{:S(2)}) async-start(), calls=%async_computation.16 | async-start | bytes 589824
  86.8 399.7 %copy-start.3 = (bf16[64,64]{1,0:T(8,128)(2,1)S(1)}, bf16[64,64]{1,0:T(8,128)(2,1)}, u32[]{:S(2)}) copy-start(bf16[64,64]{1,0:T(8,128)(2,1)} %param.27) | copy-start | bytes 24580
  86.8 399.6 %copy-start.6 = (f32[64]{0:T(128)S(1)}, f32[64]{0:T(128)}, u32[]{:S(2)}) copy-start(f32[64]{0:T(128)} %param.28) | copy-start | bytes 772
  490.5 2.5 copy-start.5
  490.5 2.5 copy-start.15
  498.7 82.5 %copy-start.13 = (bf16[512,64]{0,1:T(8,128)(2,1)S(1)}, bf16[512,64]{0,1:T(8,128)(2,1)}, u32[]{:S(2)}) copy-start(bf16[512,64]{0,1:T(8,128)(2,1)} %param.32) | copy-start | bytes 196612
  498.7 297.0 %reduce-scatter.13.cloned.1.call-start = ((), (), s32[]{:S(2)}) async-start(), calls=%async_computation.13 | async-start | bytes 589824
  581.2 2.4 copy-start.16
  583.6 2.4 copy-start.18
  588.3 128.4 %copy-start.12 = (bf16[512,64]{0,1:T(8,128)(2,1)S(1)}, bf16[512,64]{0,1:T(8,128)(2,1)}, u32[]{:S(2)}) copy-start(bf16[512,64]{0,1:T(8,128)(2,1)} %param.33) | copy-start | bytes 196612
  589.4 246.7 %reduce-scatter.15.cloned.1.call-start = ((), (), s32[]{:S(2)}) async-start(), calls=%async_computation.14 | async-start | bytes 589824
  716.7 2.4 copy-start.11
  725.2 1.3 copy-start.10
  726.2 2.3 copy-start.14
  726.3 150.9 %reduce-scatter.17.cloned.1.call-start = ((), (), s32[]{:S(2)}) async-start(), calls=%async_computation.15 | async-start | bytes 589824
  728.5 2.1 copy-start.17
  730.6 2.1 copy-start.19
  735.8 288.5 %all-gather.14.cloned.1.call-start = ((), (), s32[]{:S(2)}) async-start(), calls=%async_computation.6 | async-start | bytes 1064960 | tf_op jit(solution)/shard_map/all_gather | solution.py:164
  878.7 1.6 copy-start.1
  884.3 2.3 copy-start.8
  884.3 2.3 copy-start.9
  887.4 274.9 %all-gather.18.cloned.1.call-start = ((), (), s32[]{:S(2)}) async-start(), calls=%async_computation.8 | async-start | bytes 1064960 | tf_op jit(solution)/shard_map/all_gather | solution.py:164
  888.1 412.0 %all-gather.22.cloned.1.call-start = ((), (), s32[]{:S(2)}) async-start(), calls=%async_computation.10 | async-start | bytes 1064960 | tf_op jit(solution)/shard_map/all_gather | solution.py:164
  888.7 549.4 %all-gather.26.cloned.1.call-start = ((), (), s32[]{:S(2)}) async-start(), calls=%async_computation.12 | async-start | bytes 1064960 | tf_op jit(solution)/shard_map/all_gather | solution.py:164
Sparse Core Ops, SparseCore 0:
  25.2 139.6 all-gather.23
  167.9 134.9 all-gather.19
  305.8 135.0 all-gather.11
  443.7 135.1 all-gather.9
  581.6 134.9 all-gather.15
  719.3 35.6 reduce-scatter.18
  758.1 37.5 reduce-scatter.12
  798.5 37.5 reduce-scatter.14
  839.7 37.4 reduce-scatter.16
  887.5 136.7 all-gather.13
  1027.3 134.9 all-gather.17
  1165.1 134.9 all-gather.21
  1303.1 134.9 all-gather.25
where the time goes:
time: 1450 us
  waiting for transfers between devices  894 us (62%)
  blocking collectives  462 us (32%)
  matrix products  51.8 us (4%)
  between operations  14.7 us (1%)
    all_gather x4, waiting for transfers between devices, per_device(): lax.all_gather(gated, 'wide', axis=2, tiled=True)  544 us
    all_gather x4, blocking collectives, per_device(): prepare_small_all = lax.all_gather(small, 'wide', axis=0, tiled=True)  399 us
    all_gather x4, waiting for transfers between devices, per_device(): prepare_normed_all = lax.all_gather(normed, 'wide', axis=0, tiled=True)  207 us
    unnamed x17, waiting for transfers between devices  143 us
    dot_general x16, matrix products, per_device(): jnp.einsum('smd,de->sme', mixed_input, weights[selector_index], preferred...  35.4 us
  transfers between devices with their start and end apart: 13, of which 10 were waited for; matrix products, arithmetic and copies ran while one was open for 4% of the time, Pallas kernels for 0%

commit v1 on v0

v1 whole, which is shorter than its diff:
```python
import jax
import jax.numpy as jnp
from jax import lax
from jax.sharding import PartitionSpec as P

CHANNEL_SPAN = 64
FEATURE_EXTENT = 4096


def per_device(
    sublevel_symbol_entries,
    prior_symbol_memory,
    entry_scaling_multiplier,
    entry_scaling_offset,
    learned_blending,
    blending_lowering_coefficients,
    blending_raising_coefficients,
    fading_lowering_coefficients,
    fading_raising_coefficients,
    learned_fading,
    immediate_item_premium,
    acceptor_projection,
    lookup_projection,
    payload_projection,
    gating_projection,
    emission_projection,
    group_scaling_multiplier,
    group_scaling_offset,
    dialogue_group_memory,
):
    rank = blending_raising_coefficients.shape[1]
    narrow_rows = dialogue_group_memory.shape[1]
    local_width = emission_projection.shape[1]
    group_partition = local_width // CHANNEL_SPAN
    sessions, steps, features = sublevel_symbol_entries.shape
    weights = (acceptor_projection, lookup_projection, payload_projection, gating_projection)

    floats = sublevel_symbol_entries.astype(jnp.float32)
    stats = lax.psum(
        jnp.stack([jnp.sum(floats, -1), jnp.sum(floats * floats, -1)], 0), "narrow"
    )
    center = stats[0][..., None] / FEATURE_EXTENT
    spread = stats[1][..., None] / FEATURE_EXTENT - center * center
    normed = (
        (floats - center) * lax.rsqrt(spread + 1e-05) * entry_scaling_multiplier
        + entry_scaling_offset
    ).astype(jnp.bfloat16)
    previous = jnp.concatenate([prior_symbol_memory[:, None], normed[:, :-1]], 1)
    normalized_float = normed.astype(jnp.float32)
    shifted_input = previous.astype(jnp.float32) - normalized_float
    blended = (normalized_float + shifted_input * learned_blending[0]).astype(jnp.bfloat16)
    partial_mix = jnp.einsum(
        "smd,dr->smr", blended, blending_lowering_coefficients,
        preferred_element_type=jnp.float32,
    )
    hidden_activation = jnp.tanh(lax.psum(partial_mix, "narrow")).astype(jnp.bfloat16)
    decay_shift = jnp.einsum(
        "smr,rd->smd", hidden_activation[..., :rank], blending_raising_coefficients[0],
        preferred_element_type=jnp.float32,
    )
    decay_mix = (
        normalized_float + shifted_input * (learned_blending[1] + decay_shift)
    ).astype(jnp.bfloat16)
    partial_decay = jnp.einsum(
        "smd,dr->smr", decay_mix, fading_lowering_coefficients,
        preferred_element_type=jnp.float32,
    )
    decay_hidden = jnp.tanh(lax.psum(partial_decay, "narrow")).astype(jnp.bfloat16)
    small = jnp.concatenate([hidden_activation[..., rank:], decay_hidden], -1)
    small_width = small.shape[-1]

    packed = jnp.concatenate(
        [
            normed.reshape(sessions, steps * features),
            prior_symbol_memory,
            small.reshape(sessions, steps * small_width),
        ],
        -1,
    )
    packed_all = lax.all_gather(packed, "wide", axis=0, tiled=True)
    all_sessions = packed_all.shape[0]
    normed_all = packed_all[:, : steps * features].reshape(all_sessions, steps, features)
    prior_all = packed_all[:, steps * features : (steps + 1) * features]
    small_all = packed_all[:, (steps + 1) * features :].reshape(
        all_sessions, steps, small_width
    )
    previous_all = jnp.concatenate([prior_all[:, None], normed_all[:, :-1]], 1)
    normalized_all = normed_all.astype(jnp.float32)
    shifted_all = previous_all.astype(jnp.float32) - normalized_all
    term_results = []
    for selector_index in range(4):
        low_rank_update = jnp.einsum(
            "smr,rd->smd",
            small_all[..., selector_index * rank : (selector_index + 1) * rank],
            blending_raising_coefficients[selector_index + 1],
            preferred_element_type=jnp.float32,
        )
        mixed_input = (
            normalized_all
            + shifted_all * (learned_blending[selector_index + 2] + low_rank_update)
        ).astype(jnp.bfloat16)
        term_results.append(
            jnp.einsum(
                "smd,de->sme", mixed_input, weights[selector_index],
                preferred_element_type=jnp.float32,
            ).astype(jnp.bfloat16)
        )
    projected = lax.psum_scatter(
        jnp.concatenate(term_results, -1), "narrow", scatter_dimension=0, tiled=True
    ).astype(jnp.float32)

    rows_start = lax.axis_index("narrow") * narrow_rows
    decay_rows = lax.dynamic_slice_in_dim(small_all[..., 4 * rank :], rows_start, narrow_rows, 0)
    decay_log = learned_fading + jnp.einsum(
        "smr,rd->smd", decay_rows, fading_raising_coefficients,
        preferred_element_type=jnp.float32,
    )
    shrink_coefficient = jnp.exp(-jnp.exp(decay_log))

    def channel_set_first(block):
        return block.reshape(narrow_rows, group_partition, CHANNEL_SPAN).transpose(1, 2, 0)

    state = dialogue_group_memory.reshape(group_partition, CHANNEL_SPAN, CHANNEL_SPAN, narrow_rows)
    reward = immediate_item_premium.reshape(group_partition, CHANNEL_SPAN)
    pieces = []
    for index in range(steps):
        acceptor = channel_set_first(projected[:, index, :local_width])
        key_now = channel_set_first(projected[:, index, local_width : 2 * local_width])
        value_now = channel_set_first(projected[:, index, 2 * local_width : 3 * local_width])
        gate_now = projected[:, index, 3 * local_width :]
        forget_now = channel_set_first(shrink_coefficient[:, index])
        dyadic = key_now[:, :, None, :] * value_now[:, None, :, :]
        retrieval = jnp.sum(
            acceptor[:, :, None, :] * (state + reward[:, :, None, None] * dyadic), 1
        )
        state = forget_now[:, :, None, :] * state + dyadic
        center_r = jnp.mean(retrieval, 1, keepdims=True)
        offset = retrieval - center_r
        scaled = offset * lax.rsqrt(jnp.mean(offset * offset, 1, keepdims=True) + 0.00064)
        squashed = scaled.transpose(2, 0, 1).reshape(narrow_rows, local_width)
        pieces.append(
            (
                (squashed * group_scaling_multiplier + group_scaling_offset)
                * jax.nn.silu(gate_now)
            ).astype(jnp.bfloat16)
        )
    gated = jnp.stack(pieces, 1)
    mixing_output = jnp.einsum(
        "smc,ce->sme",
        lax.all_gather(gated, "wide", axis=2, tiled=True),
        emission_projection,
        preferred_element_type=jnp.float32,
    ).astype(jnp.bfloat16)
    return (
        mixing_output,
        state.reshape(group_partition * CHANNEL_SPAN * CHANNEL_SPAN, narrow_rows),
    )


def solution(mesh):
    placed = (
        P("wide", None, "narrow"),
        P("wide", "narrow"),
        P("narrow"),
        P("narrow"),
        P(None, "narrow"),
        P("narrow", None),
        P(None, None, "narrow"),
        P("narrow", None),
        P(None, "wide"),
        P("wide"),
        P("wide"),
        P("narrow", "wide"),
        P("narrow", "wide"),
        P("narrow", "wide"),
        P("narrow", "wide"),
        P(None, "wide"),
        P("wide"),
        P("wide"),
        P("wide", "narrow"),
    )
    return jax.shard_map(
        per_device,
        mesh=mesh,
        in_specs=placed,
        out_specs=(P("narrow", None, "wide"), P("wide", "narrow")),
        check_vma=False,
    )
```

time: 1450 us -> 495 us (0.34)
  waiting for transfers between devices: 894 us -> 333 us
  blocking collectives: 462 us -> 62.4 us
  local copies, waits for them, and re-layouts: 12.5 us -> 33.5 us
  matrix products: 51.8 us -> 34.5 us
    all_gather x4 -> x1, waiting for transfers between devices: 544 us -> 144 us  [per_device(): lax.all_gather(gated, 'wide', axis=2, tiled=True)]
    all_gather x4 -> x0, blocking collectives: 399 us -> none  [per_device(): prepare_small_all = lax.all_gather(small, 'wide', axis=0, tiled=True)]
    unnamed x17 -> x4, waiting for transfers between devices: 143 us -> 36.1 us
    all_gather x5 -> x1, waiting for transfers between devices: 207 us -> 153 us  [per_device(): packed_all = lax.all_gather(packed, 'wide', axis=0, tiled=True)]
    dot_general x16 -> x4, matrix products: 35.4 us -> 28.3 us  [per_device(): jnp.einsum('smd,de->sme', mixed_input, weights[selector_index], preferred...]
  transfers between devices with their start and end apart: 13 -> 3, of which waited for: 10 -> 3; matrix products, arithmetic and copies ran while one was open for 4% -> 0% of each run, Pallas kernels for 0% -> 0%
where the time goes in v1:
time: 495 us; the launch traced here: 492 us
  waiting for transfers between devices  333 us (67%)
  blocking collectives  62.4 us (13%)
  matrix products  34.5 us (7%)
  local copies, waits for them, and re-layouts  33.5 us (7%)
  other arithmetic  14.3 us (3%)
  between operations  14 us (3%)
    all_gather x1, waiting for transfers between devices, per_device(): packed_all = lax.all_gather(packed, 'wide', axis=0, tiled=True)  153 us
    all_gather x1, waiting for transfers between devices, per_device(): lax.all_gather(gated, 'wide', axis=2, tiled=True)  144 us
    unnamed x4, waiting for transfers between devices  36.1 us
    dot_general x4, matrix products, per_device(): jnp.einsum('smd,de->sme', mixed_input, weights[selector_index], preferred...  28.3 us
    psum x1, blocking collectives, per_device(): lax.psum(partial_mix, 'narrow')  23.9 us
    psum x1, blocking collectives, per_device(): lax.psum(partial_decay, 'narrow')  23.6 us
    psum x1, blocking collectives, per_device(): lax.psum(jnp.stack([jnp.sum(floats, -1), jnp.sum(floats * floats, -1)], 0...  14.9 us
    unnamed x29, local copies, waits for them, and re-layouts  11.8 us
  transfers between devices with their start and end apart: 3, of which 3 were waited for; matrix products, arithmetic and copies ran while one was open for 0% of the time, Pallas kernels for 0%

profile of v1, /device:TPU:6, one launch (start us, length us, event | category | flops | bytes accessed | tf_op | source)
XLA Modules:
  0.0 491.9 jit_solution(11728200815395826238)
XLA Ops:
  7.2 0.0 copy-start
  7.2 0.0 all-gather.3.cloned.1.call-start
  7.2 1.0 convert_reduce_fusion
  8.2 14.9 %psum.21 = f32[2,16,4]{1,2,0:T(4,128)S(1)} all-reduce(f32[2,16,4]{1,2,0:T(4,128)S(1)} %pad_maximum_fusion.8), channel_id=1, replica_groups=mesh['wide'=64,'narrow'=8] {'narrow'}, use_global_device_ids=true, to_apply=%region_2.0 | all-reduce | flops 128 | bytes 1024 | tf_op jit(solution)/shard_map/psum | solution.py:39
  23.1 1.0 fusion.83
  24.1 1.0 fusion.144
  25.1 1.0 fusion.142
  26.0 1.1 fusion.77
  27.2 23.9 %psum.22 = f32[16,4,160]{2,0,1:T(8,128)S(1)} all-reduce(f32[16,4,160]{2,0,1:T(8,128)S(1)} %fusion.77), channel_id=1, replica_groups=mesh['wide'=64,'narrow'=8] {'narrow'}, use_global_device_ids=true, to_apply=%region_3.0 | all-reduce | flops 10240 | bytes 81920 | tf_op jit(solution)/shard_map/psum | solution.py:56
  51.1 0.1 slice.183
  51.2 1.1 fusion.66
  52.4 23.6 %psum.23 = f32[16,4,64]{2,0,1:T(8,128)S(1)} all-reduce(f32[16,4,64]{2,0,1:T(8,128)S(1)} %fusion.66), channel_id=1, replica_groups=mesh['wide'=64,'narrow'=8] {'narrow'}, use_global_device_ids=true, to_apply=%region_4.0 | all-reduce | flops 4096 | bytes 32768 | tf_op jit(solution)/shard_map/psum | solution.py:68
  76.0 0.1 reshape.691
  76.1 1.4 pad_maximum_fusion.2
  77.5 0.0 all-gather.3.cloned.1.call-update
  77.5 0.0 reduce-scatter.4.cloned.1.call-start
  77.6 153.2 %all-gather.3.cloned.1.call-done = bf16[1024,3328]{1,0:T(8,128)(2,1)} async-done(((bf16[16,3328]{1,0:T(8,128)(2,1)}), bf16[1024,3328]{1,0:T(8,128)(2,1)}) %all-gather.3.cloned.1.call-update) | async-done | bytes 6815760 | tf_op jit(solution)/shard_map/all_gather | solution.py:80
  230.8 4.8 slice.185
  235.6 6.4 %copy.73 = bf16[1024,2048]{0,1:T(8,128)(2,1)} copy(bf16[1024,2048]{1,0:T(8,128)(2,1)} %slice.185) | data formatting | bytes 8388608
  242.0 6.2 %copy.61 = bf16[1024,4,512]{2,0,1:T(8,128)(2,1)} copy(bf16[1024,4,512]{0,2,1:T(8,128)(2,1)} %bitcast.283) | data formatting | bytes 8388608 | tf_op jit(solution)/shard_map/reshape | solution.py:82
  248.2 0.0 slice-start
  248.2 1.4 slice-done
  249.6 1.6 copy.63
  251.3 3.8 slice.187
  255.1 0.0 copy-start.2
  255.1 1.4 slice_bitcast_fusion
  256.5 0.3 copy-done.2
  256.8 0.0 copy-done.8
  256.8 0.0 copy-done.9
  256.8 7.1 %fusion.57 = bf16[1024,4,64]{0,2,1:T(8,128)(2,1)} fusion(bf16[1024,4,512]{2,0,1:T(8,128)(2,1)} %copy.61, f32[512]{0:T(512)S(1)} %bitcast.300, bf16[1024,4,192]{0,2,1:T(8,128)(2,1)S(1)} %bitcast.286, bf16[512,64]{0,1:T(8,128)(2,1)S(1)} %copy-done.9, bf16[5,32,512]{2,1,0:T(8,128)(2,1)S(1)} %copy-done.8, bf16[1024,3,512]{2,0,1:T(8,128)(2,1)} %slice.187, ...), kind=kOutput, calls=%fused_computation.64 | convolution fusion | flops 419692544 | bytes 9275392 | tf_op jit(solution)/shard_map/smd,de->sme/dot_general | solution.py:103
  263.9 0.0 copy-done.10
  263.9 7.1 %fusion.54 = bf16[1024,4,64]{0,2,1:T(8,128)(2,1)} fusion(bf16[1024,4,512]{2,0,1:T(8,128)(2,1)} %copy.61, f32[512]{0:T(512)S(1)} %bitcast.299, bf16[1024,4,192]{0,2,1:T(8,128)(2,1)S(1)} %bitcast.287, bf16[512,64]{0,1:T(8,128)(2,1)S(1)} %copy-done.10, bf16[5,32,512]{2,1,0:T(8,128)(2,1)S(1)} %copy-done.8, bf16[1024,3,512]{2,0,1:T(8,128)(2,1)} %slice.187, ...), kind=kOutput, calls=%fused_computation.63 | convolution fusion | flops 419692544 | bytes 9275392 | tf_op jit(solution)/shard_map/smd,de->sme/dot_general | solution.py:103
  271.0 0.0 copy-done.11
  271.0 7.1 %fusion.51 = bf16[1024,4,64]{0,2,1:T(8,128)(2,1)} fusion(bf16[1024,4,512]{2,0,1:T(8,128)(2,1)} %copy.61, f32[512]{0:T(512)S(1)} %bitcast.298, bf16[1024,4,192]{0,2,1:T(8,128)(2,1)S(1)} %bitcast.288, bf16[512,64]{0,1:T(8,128)(2,1)S(1)} %copy-done.11, bf16[5,32,512]{2,1,0:T(8,128)(2,1)S(1)} %copy-done.8, bf16[1024,3,512]{2,0,1:T(8,128)(2,1)} %slice.187, ...), kind=kOutput, calls=%fused_computation.62 | convolution fusion | flops 419692544 | bytes 9275392 | tf_op jit(solution)/shard_map/smd,de->sme/dot_general | solution.py:103
  278.1 0.0 copy-done.12
  278.1 7.1 %fusion.48 = bf16[1024,4,64]{0,2,1:T(8,128)(2,1)} fusion(bf16[1024,4,512]{2,0,1:T(8,128)(2,1)} %copy.61, f32[512]{0:T(512)S(1)} %bitcast.297, bf16[1024,4,192]{0,2,1:T(8,128)(2,1)S(1)} %bitcast.289, bf16[512,64]{0,1:T(8,128)(2,1)S(1)} %copy-done.12, bf16[5,32,512]{2,1,0:T(8,128)(2,1)S(1)} %copy-done.8, bf16[1024,3,512]{2,0,1:T(8,128)(2,1)} %slice.187, ...), kind=kOutput, calls=%fused_computation.61 | convolution fusion | flops 419692544 | bytes 9275392 | tf_op jit(solution)/shard_map/smd,de->sme/dot_general | solution.py:103
  285.2 1.7 pad_maximum_fusion.1
  286.9 2.6 copy.69
  289.4 0.0 reduce-scatter.4.cloned.1.call-update
  289.4 0.3 all-gather.5.cloned.1.call-start
  289.7 0.3 copy-done.4
  290.1 0.1 mul.709
  290.1 0.1 mul.710
  290.2 1.1 slice.198
  291.3 0.0 copy-done.3
  291.3 0.0 copy-done.5
  291.3 0.2 fusion.62
  291.6 36.0 %reduce-scatter.4.cloned.1.call-done = bf16[128,1024]{1,0:T(8,128)(2,1)} async-done(((bf16[1024,1024]{1,0:T(8,128)(2,1)}), bf16[128,1024]{1,0:T(8,128)(2,1)}) %reduce-scatter.4.cloned.1.call-update) | async-done | bytes 262160
  327.6 1.1 copy.70
  328.8 0.6 broadcast_multiply_fusion.2
  329.4 0.0 copy-start.1
  329.4 0.6 broadcast_multiply_fusion
  330.1 1.0 copy-done.1
  331.0 2.1 fusion.28
  333.1 1.9 fusion.32
  335.0 2.1 fusion.47
  337.3 0.0 copy-done.6
  337.3 0.0 copy-done.7
  337.4 0.1 fusion.106
  337.5 0.6 pad_maximum_fusion.4
  338.1 0.0 all-gather.5.cloned.1.call-update
  338.1 143.6 %all-gather.5.cloned.1.call-done = bf16[128,4,4096]{0,2,1:T(8,128)(2,1)} async-done(((bf16[128,4,64]{0,2,1:T(8,128)(2,1)}), bf16[128,4,4096]{0,2,1:T(8,128)(2,1)}) %all-gather.5.cloned.1.call-update) | async-done | bytes 4194320 | tf_op jit(solution)/shard_map/all_gather | solution.py:150
  481.7 0.0 copy-done
  481.7 3.7 convolution_convert_fusion
  (34 shorter events, 0.3 us)
Async XLA Ops:
  7.2 474.6 %copy-start = (bf16[4096,64]{0,1:T(8,128)(2,1)S(1)}, bf16[4096,64]{0,1:T(8,128)(2,1)}, u32[]{:S(2)}) copy-start(bf16[4096,64]{0,1:T(8,128)(2,1)} %param.34) | copy-start | bytes 1572868
  7.2 223.6 %all-gather.3.cloned.1.call-start = ((), (), s32[]{:S(2)}) async-start(), calls=%async_computation.1 | async-start | bytes 6922240 | tf_op jit(solution)/shard_map/all_gather | solution.py:80
  77.5 250.1 %reduce-scatter.4.cloned.1.call-start = ((), (), s32[]{:S(2)}) async-start(), calls=%async_computation.3 | async-start | bytes 2359296
  248.2 1.4 slice-start
  255.1 1.7 copy-start.2
  255.1 1.7 copy-start.8
  255.1 1.7 copy-start.9
  256.8 7.1 %copy-start.10 = (bf16[512,64]{0,1:T(8,128)(2,1)S(1)}, bf16[512,64]{0,1:T(8,128)(2,1)}, u32[]{:S(2)}) copy-start(bf16[512,64]{0,1:T(8,128)(2,1)} %param.32) | copy-start | bytes 196612
  263.9 7.1 %copy-start.11 = (bf16[512,64]{0,1:T(8,128)(2,1)S(1)}, bf16[512,64]{0,1:T(8,128)(2,1)}, u32[]{:S(2)}) copy-start(bf16[512,64]{0,1:T(8,128)(2,1)} %param.31) | copy-start | bytes 196612
  271.0 7.1 %copy-start.12 = (bf16[512,64]{0,1:T(8,128)(2,1)S(1)}, bf16[512,64]{0,1:T(8,128)(2,1)}, u32[]{:S(2)}) copy-start(bf16[512,64]{0,1:T(8,128)(2,1)} %param.30) | copy-start | bytes 196612
  289.4 0.7 copy-start.4
  289.4 1.9 copy-start.3
  289.4 1.9 copy-start.5
  289.4 192.3 %all-gather.5.cloned.1.call-start = ((), (), s32[]{:S(2)}) async-start(), calls=%async_computation.2 | async-start | bytes 4259840 | tf_op jit(solution)/shard_map/all_gather | solution.py:150
  329.4 1.6 copy-start.1
  335.0 2.3 copy-start.6
  335.0 2.3 copy-start.7
Sparse Core Ops, SparseCore 0:
  77.6 153.0 all-gather.2
  289.6 38.0 reduce-scatter.3
  338.3 143.4 all-gather.4

commit v2 on v1

--- a/solution.py
+++ b/solution.py
@@ -77,7 +77,9 @@
         ],
         -1,
     )
-    packed_all = lax.all_gather(packed, "wide", axis=0, tiled=True)
+    packed_all = lax.all_gather(
+        lax.all_gather(packed, "x", axis=0, tiled=True), "z", axis=0, tiled=True
+    )
     all_sessions = packed_all.shape[0]
     normed_all = packed_all[:, : steps * features].reshape(all_sessions, steps, features)
     prior_all = packed_all[:, steps * features : (steps + 1) * features]
@@ -147,7 +149,9 @@
     gated = jnp.stack(pieces, 1)
     mixing_output = jnp.einsum(
         "smc,ce->sme",
-        lax.all_gather(gated, "wide", axis=2, tiled=True),
+        lax.all_gather(
+            lax.all_gather(gated, "x", axis=2, tiled=True), "z", axis=2, tiled=True
+        ),
         emission_projection,
         preferred_element_type=jnp.float32,
     ).astype(jnp.bfloat16)
@@ -158,31 +162,38 @@
 
 
 def solution(mesh):
+    wide_size = mesh.shape["wide"]
+    x_size = 4 if wide_size % 4 == 0 else 1
+    split = jax.sharding.Mesh(
+        mesh.devices.reshape(wide_size // x_size, x_size, mesh.shape["narrow"]),
+        ("z", "x", "narrow"),
+    )
+    wide = ("z", "x")
     placed = (
-        P("wide", None, "narrow"),
-        P("wide", "narrow"),
+        P(wide, None, "narrow"),
+        P(wide, "narrow"),
         P("narrow"),
         P("narrow"),
         P(None, "narrow"),
         P("narrow", None),
         P(None, None, "narrow"),
         P("narrow", None),
-        P(None, "wide"),
-        P("wide"),
-        P("wide"),
-        P("narrow", "wide"),
-        P("narrow", "wide"),
-        P("narrow", "wide"),
-        P("narrow", "wide"),
-        P(None, "wide"),
-        P("wide"),
-        P("wide"),
-        P("wide", "narrow"),
+        P(None, wide),
+        P(wide),
+        P(wide),
+        P("narrow", wide),
+        P("narrow", wide),
+        P("narrow", wide),
+        P("narrow", wide),
+        P(None, wide),
+        P(wide),
+        P(wide),
+        P(wide, "narrow"),
     )
     return jax.shard_map(
         per_device,
-        mesh=mesh,
+        mesh=split,
         in_specs=placed,
-        out_specs=(P("narrow", None, "wide"), P("wide", "narrow")),
+        out_specs=(P("narrow", None, wide), P(wide, "narrow")),
         check_vma=False,
     )

time: 495 us -> 410 us (0.83)
  waiting for transfers between devices: 333 us -> 223 us
  blocking collectives: 62.4 us -> 88.6 us
    all_gather x2, waiting for transfers between devices: 297 us -> 186 us  [the longest x1 94.6 us: per_device(): lax.all_gather(lax.all_gather(gated, 'x', axis=2, tiled=True), 'z', axis=...]
    all_gather x0 -> x2, blocking collectives: none -> 26.2 us  [the longest x1 14 us: per_device(): lax.all_gather(packed, 'x', axis=0, tiled=True)]
where the time goes in v2:
time: 410 us; the launch traced here: 408 us
  waiting for transfers between devices  223 us (54%)
  blocking collectives  88.6 us (22%)
  matrix products  35 us (9%)
  local copies, waits for them, and re-layouts  34.5 us (8%)
  between operations  14 us (3%)
  other arithmetic  13 us (3%)
    all_gather x1, waiting for transfers between devices, per_device(): lax.all_gather(lax.all_gather(gated, 'x', axis=2, tiled=True), 'z', axis=...  94.6 us
    all_gather x1, waiting for transfers between devices, per_device(): lax.all_gather(lax.all_gather(packed, 'x', axis=0, tiled=True), 'z', axis...  91.1 us
    unnamed x4, waiting for transfers between devices  37.3 us
    dot_general x4, matrix products, per_device(): jnp.einsum('smd,de->sme', mixed_input, weights[selector_index], preferred...  28.3 us
    psum x1, blocking collectives, per_device(): lax.psum(partial_mix, 'narrow')  23.9 us
    psum x1, blocking collectives, per_device(): lax.psum(partial_decay, 'narrow')  23.6 us
    psum x1, blocking collectives, per_device(): lax.psum(jnp.stack([jnp.sum(floats, -1), jnp.sum(floats * floats, -1)], 0...  14.9 us
    all_gather x1, blocking collectives, per_device(): lax.all_gather(packed, 'x', axis=0, tiled=True)  14 us
  transfers between devices with their start and end apart: 3, of which 3 were waited for; matrix products, arithmetic and copies ran while one was open for 0% of the time, Pallas kernels for 0%

profile of v2, /device:TPU:6, one launch (start us, length us, event | category | flops | bytes accessed | tf_op | source)
XLA Modules:
  0.0 408.4 jit_solution(14535004317118154650)
XLA Ops:
  7.2 0.0 copy-start
  7.2 0.0 all-gather.3.cloned.1.call-start
  7.2 1.0 convert_reduce_fusion
  8.2 14.9 %psum.21 = f32[2,16,4]{1,2,0:T(4,128)S(1)} all-reduce(f32[2,16,4]{1,2,0:T(4,128)S(1)} %pad_maximum_fusion.8), channel_id=1, replica_groups=mesh['z'=16,'x'=4,'narrow'=8] {'narrow'}, use_global_device_ids=true, to_apply=%region_2.0 | all-reduce | flops 128 | bytes 1024 | tf_op jit(solution)/shard_map/psum | solution.py:39
  23.1 1.0 fusion.83
  24.1 1.0 fusion.144
  25.1 1.0 fusion.142
  26.0 1.1 fusion.77
  27.2 23.9 %psum.22 = f32[16,4,160]{2,0,1:T(8,128)S(1)} all-reduce(f32[16,4,160]{2,0,1:T(8,128)S(1)} %fusion.77), channel_id=1, replica_groups=mesh['z'=16,'x'=4,'narrow'=8] {'narrow'}, use_global_device_ids=true, to_apply=%region_3.0 | all-reduce | flops 10240 | bytes 81920 | tf_op jit(solution)/shard_map/psum | solution.py:56
  51.1 0.1 slice.183
  51.2 1.1 fusion.66
  52.4 23.6 %psum.23 = f32[16,4,64]{2,0,1:T(8,128)S(1)} all-reduce(f32[16,4,64]{2,0,1:T(8,128)S(1)} %fusion.66), channel_id=1, replica_groups=mesh['z'=16,'x'=4,'narrow'=8] {'narrow'}, use_global_device_ids=true, to_apply=%region_4.0 | all-reduce | flops 4096 | bytes 32768 | tf_op jit(solution)/shard_map/psum | solution.py:68
  76.0 0.1 reshape.691
  76.1 0.7 pad_maximum_fusion.2
  76.8 14.0 %all_gather.12 = bf16[64,3328]{1,0:T(8,128)(2,1)} all-gather(bf16[16,3328]{1,0:T(8,128)(2,1)S(1)} %pad_maximum_fusion.2), channel_id=1, replica_groups=mesh['z'=16,'x'=4,'narrow'=8] {'x'}, dimensions={0}, use_global_device_ids=true | all-gather | bytes 532480 | tf_op jit(solution)/shard_map/all_gather | solution.py:81
  90.8 0.0 all-gather.3.cloned.1.call-update
  90.8 0.0 reduce-scatter.4.cloned.1.call-start
  90.9 91.1 %all-gather.3.cloned.1.call-done = bf16[1024,3328]{1,0:T(8,128)(2,1)} async-done(((bf16[64,3328]{1,0:T(8,128)(2,1)}), bf16[1024,3328]{1,0:T(8,128)(2,1)}) %all-gather.3.cloned.1.call-update) | async-done | bytes 6815760 | tf_op jit(solution)/shard_map/all_gather | solution.py:80
  182.0 4.8 %slice.185 = bf16[1024,2048]{1,0:T(8,128)(2,1)} slice(bf16[1024,3328]{1,0:T(8,128)(2,1)} %all-gather.3.cloned.1.call-done), slice={[0:1024], [0:2048]} | slice | bytes 8388608 | tf_op jit(solution)/shard_map/slice | solution.py:84
  186.8 6.4 %copy.139 = bf16[1024,2048]{0,1:T(8,128)(2,1)} copy(bf16[1024,2048]{1,0:T(8,128)(2,1)} %slice.185) | data formatting | bytes 8388608
  193.2 6.2 %copy.125 = bf16[1024,4,512]{2,0,1:T(8,128)(2,1)} copy(bf16[1024,4,512]{0,2,1:T(8,128)(2,1)} %bitcast.283) | data formatting | bytes 8388608 | tf_op jit(solution)/shard_map/reshape | solution.py:84
  199.4 1.4 slice-done
  200.9 1.6 copy.127
  202.5 3.8 slice.187
  206.3 1.4 slice_bitcast_fusion
  207.8 0.3 copy-done.2
  208.1 0.0 copy-done.8
  208.1 0.0 copy-done.9
  208.1 7.1 %fusion.57 = bf16[1024,4,64]{0,2,1:T(8,128)(2,1)} fusion(bf16[1024,4,512]{2,0,1:T(8,128)(2,1)} %copy.125, f32[512]{0:T(512)S(1)} %bitcast.300, bf16[1024,4,192]{0,2,1:T(8,128)(2,1)S(1)} %bitcast.286, bf16[512,64]{0,1:T(8,128)(2,1)S(1)} %copy-done.9, bf16[5,32,512]{2,1,0:T(8,128)(2,1)S(1)} %copy-done.8, bf16[1024,3,512]{2,0,1:T(8,128)(2,1)} %slice.187, ...), kind=kOutput, calls=%fused_computation.64 | convolution fusion | flops 419692544 | bytes 9275392 | tf_op jit(solution)/shard_map/smd,de->sme/dot_general | solution.py:105
  215.1 0.0 copy-done.10
  215.1 7.1 %fusion.54 = bf16[1024,4,64]{0,2,1:T(8,128)(2,1)} fusion(bf16[1024,4,512]{2,0,1:T(8,128)(2,1)} %copy.125, f32[512]{0:T(512)S(1)} %bitcast.299, bf16[1024,4,192]{0,2,1:T(8,128)(2,1)S(1)} %bitcast.287, bf16[512,64]{0,1:T(8,128)(2,1)S(1)} %copy-done.10, bf16[5,32,512]{2,1,0:T(8,128)(2,1)S(1)} %copy-done.8, bf16[1024,3,512]{2,0,1:T(8,128)(2,1)} %slice.187, ...), kind=kOutput, calls=%fused_computation.63 | convolution fusion | flops 419692544 | bytes 9275392 | tf_op jit(solution)/shard_map/smd,de->sme/dot_general | solution.py:105
  222.2 0.0 copy-done.11
  222.2 7.1 %fusion.51 = bf16[1024,4,64]{0,2,1:T(8,128)(2,1)} fusion(bf16[1024,4,512]{2,0,1:T(8,128)(2,1)} %copy.125, f32[512]{0:T(512)S(1)} %bitcast.298, bf16[1024,4,192]{0,2,1:T(8,128)(2,1)S(1)} %bitcast.288, bf16[512,64]{0,1:T(8,128)(2,1)S(1)} %copy-done.11, bf16[5,32,512]{2,1,0:T(8,128)(2,1)S(1)} %copy-done.8, bf16[1024,3,512]{2,0,1:T(8,128)(2,1)} %slice.187, ...), kind=kOutput, calls=%fused_computation.62 | convolution fusion | flops 419692544 | bytes 9275392 | tf_op jit(solution)/shard_map/smd,de->sme/dot_general | solution.py:105
  229.3 0.0 copy-done.12
  229.3 7.1 %fusion.48 = bf16[1024,4,64]{0,2,1:T(8,128)(2,1)} fusion(bf16[1024,4,512]{2,0,1:T(8,128)(2,1)} %copy.125, f32[512]{0:T(512)S(1)} %bitcast.297, bf16[1024,4,192]{0,2,1:T(8,128)(2,1)S(1)} %bitcast.289, bf16[512,64]{0,1:T(8,128)(2,1)S(1)} %copy-done.12, bf16[5,32,512]{2,1,0:T(8,128)(2,1)S(1)} %copy-done.8, bf16[1024,3,512]{2,0,1:T(8,128)(2,1)} %slice.187, ...), kind=kOutput, calls=%fused_computation.61 | convolution fusion | flops 419692544 | bytes 9275392 | tf_op jit(solution)/shard_map/smd,de->sme/dot_general | solution.py:105
  236.4 1.7 pad_maximum_fusion.1
  238.1 2.6 copy.135
  240.6 0.0 reduce-scatter.4.cloned.1.call-update
  240.7 0.3 all-gather.5.cloned.1.call-start
  240.9 0.3 copy-done.4
  241.3 0.1 mul.709
  241.4 0.1 mul.710
  241.4 1.1 slice.198
  242.5 0.0 copy-done.3
  242.5 0.0 copy-done.5
  242.5 0.2 fusion.62
  242.8 37.2 %reduce-scatter.4.cloned.1.call-done = bf16[128,1024]{1,0:T(8,128)(2,1)} async-done(((bf16[1024,1024]{1,0:T(8,128)(2,1)}), bf16[128,1024]{1,0:T(8,128)(2,1)}) %reduce-scatter.4.cloned.1.call-update) | async-done | bytes 262160
  280.0 1.1 copy.136
  281.2 0.6 broadcast_multiply_fusion.2
  281.8 0.0 copy-start.1
  281.8 0.6 broadcast_multiply_fusion
  282.5 1.0 copy-done.1
  283.4 2.1 fusion.28
  285.5 1.9 fusion.32
  287.4 2.1 fusion.47
  289.7 0.0 copy-done.6
  289.8 0.0 copy-done.7
  289.8 0.1 fusion.106
  289.9 0.1 copy.129
  290.0 12.3 %all_gather.14 = bf16[128,4,256]{0,1,2:T(4,128)(2,1)S(1)} all-gather(bf16[128,4,64]{0,1,2:T(4,128)(2,1)S(1)} %copy.129), channel_id=1, replica_groups=mesh['z'=16,'x'=4,'narrow'=8] {'x'}, dimensions={2}, use_global_device_ids=true | all-gather | bytes 327680 | tf_op jit(solution)/shard_map/all_gather | solution.py:153
  302.2 0.9 copy.130
  303.1 0.0 all-gather.5.cloned.1.call-update
  303.1 94.6 %all-gather.5.cloned.1.call-done = bf16[128,4,4096]{2,0,1:T(8,128)(2,1)} async-done(((bf16[128,4,256]{2,0,1:T(8,128)(2,1)}), bf16[128,4,4096]{2,0,1:T(8,128)(2,1)}) %all-gather.5.cloned.1.call-update) | async-done | bytes 4194320 | tf_op jit(solution)/shard_map/all_gather | solution.py:152
  397.7 4.2 %convolution_convert_fusion = bf16[128,4,64]{0,2,1:T(8,128)(2,1)} fusion(bf16[128,4,4096]{2,0,1:T(8,128)(2,1)} %all-gather.5.cloned.1.call-done, bf16[4096,64]{0,1:T(8,128)(2,1)S(1)} %copy-done), kind=kOutput, calls=%fused_computation.73 | convolution fusion | flops 268468224 | bytes 4784128 | tf_op jit(solution)/shard_map/smc,ce->sme/dot_general | solution.py:150
  (38 shorter events, 0.4 us)
Async XLA Ops:
  7.2 390.5 %copy-start = (bf16[4096,64]{0,1:T(8,128)(2,1)S(1)}, bf16[4096,64]{0,1:T(8,128)(2,1)}, u32[]{:S(2)}) copy-start(bf16[4096,64]{0,1:T(8,128)(2,1)} %param.34) | copy-start | bytes 1572868
  7.2 174.8 %all-gather.3.cloned.1.call-start = ((), (), s32[]{:S(2)}) async-start(), calls=%async_computation.1 | async-start | bytes 7241728 | tf_op jit(solution)/shard_map/all_gather | solution.py:80
  90.8 189.2 %reduce-scatter.4.cloned.1.call-start = ((), (), s32[]{:S(2)}) async-start(), calls=%async_computation.3 | async-start | bytes 2359296
  199.4 1.4 slice-start
  206.3 1.7 copy-start.2
  206.3 1.7 copy-start.8
  206.3 1.7 copy-start.9
  208.1 7.1 %copy-start.10 = (bf16[512,64]{0,1:T(8,128)(2,1)S(1)}, bf16[512,64]{0,1:T(8,128)(2,1)}, u32[]{:S(2)}) copy-start(bf16[512,64]{0,1:T(8,128)(2,1)} %param.32) | copy-start | bytes 196612
  215.1 7.1 %copy-start.11 = (bf16[512,64]{0,1:T(8,128)(2,1)S(1)}, bf16[512,64]{0,1:T(8,128)(2,1)}, u32[]{:S(2)}) copy-start(bf16[512,64]{0,1:T(8,128)(2,1)} %param.31) | copy-start | bytes 196612
  222.2 7.1 %copy-start.12 = (bf16[512,64]{0,1:T(8,128)(2,1)S(1)}, bf16[512,64]{0,1:T(8,128)(2,1)}, u32[]{:S(2)}) copy-start(bf16[512,64]{0,1:T(8,128)(2,1)} %param.30) | copy-start | bytes 196612
  240.6 0.7 copy-start.4
  240.6 1.9 copy-start.3
  240.6 1.9 copy-start.5
  240.7 157.0 %all-gather.5.cloned.1.call-start = ((), (), s32[]{:S(2)}) async-start(), calls=%async_computation.2 | async-start | bytes 4456448 | tf_op jit(solution)/shard_map/all_gather | solution.py:152
  281.8 1.6 copy-start.1
  287.4 2.3 copy-start.6
  287.4 2.3 copy-start.7
Sparse Core Ops, SparseCore 0:
  91.0 90.9 all-gather.2
  240.8 39.1 reduce-scatter.3
  303.2 94.4 all-gather.4

commit v3 on v2

--- a/solution.py
+++ b/solution.py
@@ -70,49 +70,44 @@
     small_width = small.shape[-1]
 
     packed = jnp.concatenate(
-        [
-            normed.reshape(sessions, steps * features),
-            prior_symbol_memory,
-            small.reshape(sessions, steps * small_width),
-        ],
+        [prior_symbol_memory]
+        + [normed[:, index] for index in range(steps)]
+        + [small.reshape(sessions, steps * small_width)],
         -1,
     )
     packed_all = lax.all_gather(
         lax.all_gather(packed, "x", axis=0, tiled=True), "z", axis=0, tiled=True
     )
-    all_sessions = packed_all.shape[0]
-    normed_all = packed_all[:, : steps * features].reshape(all_sessions, steps, features)
-    prior_all = packed_all[:, steps * features : (steps + 1) * features]
-    small_all = packed_all[:, (steps + 1) * features :].reshape(
-        all_sessions, steps, small_width
-    )
-    previous_all = jnp.concatenate([prior_all[:, None], normed_all[:, :-1]], 1)
-    normalized_all = normed_all.astype(jnp.float32)
-    shifted_all = previous_all.astype(jnp.float32) - normalized_all
+    small_start = (steps + 1) * features
     term_results = []
-    for selector_index in range(4):
-        low_rank_update = jnp.einsum(
-            "smr,rd->smd",
-            small_all[..., selector_index * rank : (selector_index + 1) * rank],
-            blending_raising_coefficients[selector_index + 1],
-            preferred_element_type=jnp.float32,
-        )
-        mixed_input = (
-            normalized_all
-            + shifted_all * (learned_blending[selector_index + 2] + low_rank_update)
-        ).astype(jnp.bfloat16)
-        term_results.append(
-            jnp.einsum(
-                "smd,de->sme", mixed_input, weights[selector_index],
+    for index in range(steps):
+        previous_now = packed_all[:, index * features : (index + 1) * features]
+        normed_now = packed_all[:, (index + 1) * features : (index + 2) * features]
+        normalized_now = normed_now.astype(jnp.float32)
+        shifted_now = previous_now.astype(jnp.float32) - normalized_now
+        small_now = small_start + index * small_width
+        for selector_index in range(4):
+            low_rank_update = jnp.dot(
+                packed_all[:, small_now + selector_index * rank : small_now + (selector_index + 1) * rank],
+                blending_raising_coefficients[selector_index + 1],
                 preferred_element_type=jnp.float32,
+            )
+            mixed_input = (
+                normalized_now
+                + shifted_now * (learned_blending[selector_index + 2] + low_rank_update)
             ).astype(jnp.bfloat16)
-        )
+            term_results.append(
+                jnp.dot(
+                    mixed_input, weights[selector_index], preferred_element_type=jnp.float32
+                ).astype(jnp.bfloat16)
+            )
     projected = lax.psum_scatter(
         jnp.concatenate(term_results, -1), "narrow", scatter_dimension=0, tiled=True
-    ).astype(jnp.float32)
+    ).astype(jnp.float32).reshape(narrow_rows, steps, 4 * local_width)
 
     rows_start = lax.axis_index("narrow") * narrow_rows
-    decay_rows = lax.dynamic_slice_in_dim(small_all[..., 4 * rank :], rows_start, narrow_rows, 0)
+    own_rows = lax.dynamic_slice_in_dim(packed_all[:, small_start:], rows_start, narrow_rows, 0)
+    decay_rows = own_rows.reshape(narrow_rows, steps, small_width)[..., 4 * rank :]
     decay_log = learned_fading + jnp.einsum(
         "smr,rd->smd", decay_rows, fading_raising_coefficients,
         preferred_element_type=jnp.float32,
@@ -146,15 +141,17 @@
                 * jax.nn.silu(gate_now)
             ).astype(jnp.bfloat16)
         )
-    gated = jnp.stack(pieces, 1)
-    mixing_output = jnp.einsum(
-        "smc,ce->sme",
-        lax.all_gather(
-            lax.all_gather(gated, "x", axis=2, tiled=True), "z", axis=2, tiled=True
-        ),
-        emission_projection,
-        preferred_element_type=jnp.float32,
-    ).astype(jnp.bfloat16)
+    gated = jnp.stack(pieces, 1).reshape(narrow_rows * steps, local_width).T
+    gated_all = lax.all_gather(
+        lax.all_gather(gated, "x", axis=0, tiled=True), "z", axis=0, tiled=True
+    )
+    mixing_output = (
+        jnp.einsum(
+            "cs,ce->se", gated_all, emission_projection, preferred_element_type=jnp.float32
+        )
+        .astype(jnp.bfloat16)
+        .reshape(narrow_rows, steps, local_width)
+    )
     return (
         mixing_output,
         state.reshape(group_partition * CHANNEL_SPAN * CHANNEL_SPAN, narrow_rows),

time: 410 us -> 374 us (0.912)
  local copies, waits for them, and re-layouts: 34.5 us -> 9.14 us
  waiting for transfers between devices: 223 us -> 206 us
  matrix products: 35 us -> 44.3 us
    all_gather x1, waiting for transfers between devices: 94.6 us -> 77.6 us  [per_device(): lax.all_gather(lax.all_gather(gated, 'x', axis=0, tiled=True), 'z', axis=...]
    slice x6 -> x2, local copies, waits for them, and re-layouts: 12.8 us -> 0.67 us  [per_device(): packed_all[:, small_start:]]
    dot_general x5 -> x17, matrix products: 32.5 us -> 41.9 us  [the longest x16 38.8 us: per_device(): jnp.dot(mixed_input, weights[selector_index], preferred_element_type=jnp....]
    reshape x2 -> x0, local copies, waits for them, and re-layouts: 6.22 us -> none  [the longest x1 6.22 us: per_device(): packed_all[:, :steps * features].reshape(all_sessions, steps, features)]
    unnamed x29 -> x32, local copies, waits for them, and re-layouts: 11.8 us -> 6.55 us
where the time goes in v3:
time: 374 us; the launch traced here: 373 us
  waiting for transfers between devices  206 us (55%)
  blocking collectives  89.4 us (24%)
  matrix products  44.3 us (12%)
  between operations  14.3 us (4%)
  other arithmetic  9.65 us (3%)
  local copies, waits for them, and re-layouts  9.14 us (2%)
    all_gather x1, waiting for transfers between devices, per_device(): lax.all_gather(lax.all_gather(packed, 'x', axis=0, tiled=True), 'z', axis...  91.1 us
    all_gather x1, waiting for transfers between devices, per_device(): lax.all_gather(lax.all_gather(gated, 'x', axis=0, tiled=True), 'z', axis=...  77.6 us
    dot_general x16, matrix products, per_device(): jnp.dot(mixed_input, weights[selector_index], preferred_element_type=jnp....  38.8 us
    unnamed x4, waiting for transfers between devices  37.5 us
    psum x1, blocking collectives, per_device(): lax.psum(partial_mix, 'narrow')  23.9 us
    psum x1, blocking collectives, per_device(): lax.psum(partial_decay, 'narrow')  23.6 us
    psum x1, blocking collectives, per_device(): lax.psum(jnp.stack([jnp.sum(floats, -1), jnp.sum(floats * floats, -1)], 0...  14.9 us
    all_gather x1, blocking collectives, per_device(): lax.all_gather(packed, 'x', axis=0, tiled=True)  14 us
  transfers between devices with their start and end apart: 3, of which 3 were waited for; matrix products, arithmetic and copies ran while one was open for 0% of the time, Pallas kernels for 0%

profile of v3, /device:TPU:6, one launch (start us, length us, event | category | flops | bytes accessed | tf_op | source)
XLA Modules:
  0.0 373.3 jit_solution(8394787153175697751)
XLA Ops:
  7.2 0.0 copy-start
  7.2 0.0 copy-start.5
  7.2 0.0 all-gather.3.cloned.1.call-start
  7.2 1.0 convert_reduce_fusion
  8.3 14.9 %psum.21 = f32[2,16,4]{1,2,0:T(4,128)S(1)} all-reduce(f32[2,16,4]{1,2,0:T(4,128)S(1)} %pad_maximum_fusion.5), channel_id=1, replica_groups=mesh['z'=16,'x'=4,'narrow'=8] {'narrow'}, use_global_device_ids=true, to_apply=%region_2.0 | all-reduce | flops 128 | bytes 1024 | tf_op jit(solution)/shard_map/psum | solution.py:39
  23.2 1.0 fusion.288
  24.2 1.0 fusion.186
  25.1 0.7 constant_dynamic-update-slice_fusion.5
  25.9 1.1 fusion.180
  27.0 23.9 %psum.22 = f32[16,4,160]{2,0,1:T(8,128)S(1)} all-reduce(f32[16,4,160]{2,0,1:T(8,128)S(1)} %fusion.180), channel_id=1, replica_groups=mesh['z'=16,'x'=4,'narrow'=8] {'narrow'}, use_global_device_ids=true, to_apply=%region_3.0 | all-reduce | flops 10240 | bytes 81920 | tf_op jit(solution)/shard_map/psum | solution.py:56
  50.9 0.1 slice.286
  51.0 1.1 fusion.98
  52.2 23.6 %psum.23 = f32[16,4,64]{2,0,1:T(8,128)S(1)} all-reduce(f32[16,4,64]{2,0,1:T(8,128)S(1)} %fusion.98), channel_id=1, replica_groups=mesh['z'=16,'x'=4,'narrow'=8] {'narrow'}, use_global_device_ids=true, to_apply=%region_4.0 | all-reduce | flops 4096 | bytes 32768 | tf_op jit(solution)/shard_map/psum | solution.py:68
  75.8 0.1 reshape.692
  76.0 14.0 %all_gather.12 = bf16[64,3328]{1,0:T(8,128)(2,1)} all-gather(bf16[16,3328]{1,0:T(8,128)(2,1)S(1)} %constant_dynamic-update-slice_fusion), channel_id=1, replica_groups=mesh['z'=16,'x'=4,'narrow'=8] {'x'}, dimensions={0}, use_global_device_ids=true | all-gather | bytes 532480 | tf_op jit(solution)/shard_map/all_gather | solution.py:79
  90.0 0.0 all-gather.3.cloned.1.call-update
  90.0 0.0 reduce-scatter.4.cloned.1.call-start
  90.1 91.1 %all-gather.3.cloned.1.call-done = bf16[1024,3328]{1,0:T(8,128)(2,1)} async-done(((bf16[64,3328]{1,0:T(8,128)(2,1)}), bf16[1024,3328]{1,0:T(8,128)(2,1)}) %all-gather.3.cloned.1.call-update) | async-done | bytes 6815760 | tf_op jit(solution)/shard_map/all_gather | solution.py:78
  181.2 2.4 fusion.69
  183.5 0.0 copy-start.8
  183.5 2.5 fusion.71
  186.0 0.0 copy-start.9
  186.0 2.5 fusion.73
  188.5 2.4 fusion.75
  191.0 2.5 fusion.77
  193.5 2.4 fusion.79
  195.9 2.4 fusion.81
  198.3 2.4 fusion.83
  200.7 2.4 fusion.85
  203.1 2.4 fusion.87
  205.5 2.4 fusion.89
  208.0 2.5 fusion.91
  210.5 2.4 fusion.61
  212.9 2.4 fusion.63
  215.4 2.4 fusion.65
  217.7 2.4 fusion.67
  220.2 2.6 copy.60
  222.7 0.0 reduce-scatter.4.cloned.1.call-update
  222.8 0.0 copy-start.10
  222.8 0.2 all-gather.5.cloned.1.call-start
  223.0 0.4 copy-done.2
  223.4 0.1 mul.757
  223.5 0.1 mul.758
  223.5 0.7 slice-done
  224.2 0.2 copy.52
  224.4 0.2 fusion.94
  224.7 37.5 %reduce-scatter.4.cloned.1.call-done = bf16[128,1024]{1,0:T(8,128)(2,1)} async-done(((bf16[1024,1024]{1,0:T(8,128)(2,1)}), bf16[128,1024]{1,0:T(8,128)(2,1)}) %reduce-scatter.4.cloned.1.call-update) | async-done | bytes 262160
  262.1 1.1 copy.61
  263.3 0.6 broadcast_multiply_fusion.2
  264.0 0.0 copy-start.1
  264.0 0.6 broadcast_multiply_fusion
  264.6 1.0 copy-done.1
  265.6 2.1 fusion.8
  267.6 1.9 fusion.28
  269.6 2.1 fusion.43
  271.9 0.1 fusion.205
  272.0 0.1 copy.54
  272.2 0.1 copy.55
  272.3 13.0 %all_gather.14 = bf16[256,512]{1,0:T(8,128)(2,1)} all-gather(bf16[64,512]{1,0:T(8,128)(2,1)S(1)} %copy.55), channel_id=1, replica_groups=mesh['z'=16,'x'=4,'narrow'=8] {'x'}, dimensions={0}, use_global_device_ids=true | all-gather | bytes 327680 | tf_op jit(solution)/shard_map/all_gather | solution.py:146
  285.3 0.0 all-gather.5.cloned.1.call-update
  285.3 77.6 %all-gather.5.cloned.1.call-done = bf16[4096,512]{1,0:T(8,128)(2,1)} async-done(((bf16[256,512]{1,0:T(8,128)(2,1)}), bf16[4096,512]{1,0:T(8,128)(2,1)}) %all-gather.5.cloned.1.call-update) | async-done | bytes 4194320 | tf_op jit(solution)/shard_map/all_gather | solution.py:145
  362.9 3.0 convolution_convert_fusion
  365.9 0.1 copy.56
  366.0 0.7 copy.57
  (47 shorter events, 0.4 us)
Async XLA Ops:
  7.2 355.7 %copy-start = (bf16[4096,64]{0,1:T(8,128)(2,1)S(1)}, bf16[4096,64]{0,1:T(8,128)(2,1)}, u32[]{:S(2)}) copy-start(bf16[4096,64]{0,1:T(8,128)(2,1)} %param.34) | copy-start | bytes 1572868
  7.2 174.0 %copy-start.5 = (bf16[5,32,512]{2,1,0:T(8,128)(2,1)S(1)}, bf16[5,32,512]{2,1,0:T(8,128)(2,1)}, u32[]{:S(2)}) copy-start(bf16[5,32,512]{2,1,0:T(8,128)(2,1)} %param.25) | copy-start | bytes 491524
  7.2 174.0 %copy-start.6 = (bf16[512,64]{0,1:T(8,128)(2,1)S(1)}, bf16[512,64]{0,1:T(8,128)(2,1)}, u32[]{:S(2)}) copy-start(bf16[512,64]{0,1:T(8,128)(2,1)} %param.30) | copy-start | bytes 196612
  7.2 173.9 %all-gather.3.cloned.1.call-start = ((), (), s32[]{:S(2)}) async-start(), calls=%async_computation.1 | async-start | bytes 7241728 | tf_op jit(solution)/shard_map/all_gather | solution.py:78
  90.0 93.6 %copy-start.7 = (bf16[512,64]{0,1:T(8,128)(2,1)S(1)}, bf16[512,64]{0,1:T(8,128)(2,1)}, u32[]{:S(2)}) copy-start(bf16[512,64]{0,1:T(8,128)(2,1)} %param.31) | copy-start | bytes 196612
  90.0 172.1 %reduce-scatter.4.cloned.1.call-start = ((), (), s32[]{:S(2)}) async-start(), calls=%async_computation.3 | async-start | bytes 2359296
  183.5 2.5 copy-start.8
  186.0 2.5 copy-start.9
  222.7 0.7 copy-start.2
  222.8 1.4 slice-start
  222.8 1.6 copy-start.10
  222.8 1.6 copy-start.11
  222.8 140.1 %all-gather.5.cloned.1.call-start = ((), (), s32[]{:S(2)}) async-start(), calls=%async_computation.2 | async-start | bytes 4456448 | tf_op jit(solution)/shard_map/all_gather | solution.py:145
  264.0 1.6 copy-start.1
  269.6 2.3 copy-start.3
  269.6 2.3 copy-start.4
Sparse Core Ops, SparseCore 0:
  90.1 90.9 all-gather.2
  222.9 39.2 reduce-scatter.3
  285.4 77.4 all-gather.4

commit v4 on v3

--- a/solution.py
+++ b/solution.py
@@ -2,9 +2,83 @@
 import jax.numpy as jnp
 from jax import lax
 from jax.sharding import PartitionSpec as P
+from jax.experimental import pallas as pl
+from jax.experimental.pallas import tpu as pltpu
 
 CHANNEL_SPAN = 64
 FEATURE_EXTENT = 4096
+
+
+def narrow_sum_kernel(count, x_ref, o_ref, recv, send_sems, recv_sems):
+    me = lax.axis_index("narrow")
+    here = (lax.axis_index("z"), lax.axis_index("x"))
+
+    def peer_id(peer):
+        return here + (peer,)
+
+    barrier = pltpu.get_barrier_semaphore()
+    for peer in range(count):
+        @pl.when(peer != me)
+        def _():
+            pl.semaphore_signal(
+                barrier, 1, device_id=peer_id(peer), device_id_type=pl.DeviceIdType.MESH
+            )
+    pl.semaphore_wait(barrier, count - 1)
+
+    def outgoing(peer):
+        return pltpu.make_async_remote_copy(
+            src_ref=x_ref,
+            dst_ref=recv.at[me],
+            send_sem=send_sems.at[peer],
+            recv_sem=recv_sems.at[me],
+            device_id=peer_id(peer),
+            device_id_type=pl.DeviceIdType.MESH,
+        )
+
+    def incoming(peer):
+        return pltpu.make_async_remote_copy(
+            src_ref=x_ref,
+            dst_ref=recv.at[peer],
+            send_sem=send_sems.at[peer],
+            recv_sem=recv_sems.at[peer],
+            device_id=peer_id(peer),
+            device_id_type=pl.DeviceIdType.MESH,
+        )
+
+    for peer in range(count):
+        @pl.when(peer != me)
+        def _():
+            outgoing(peer).start()
+
+    recv[me] = x_ref[...]
+    for peer in range(count):
+        @pl.when(peer != me)
+        def _():
+            outgoing(peer).wait_send()
+            incoming(peer).wait_recv()
+
+    total = recv[0]
+    for peer in range(1, count):
+        total = total + recv[peer]
+    o_ref[...] = total
+
+
+def narrow_sum(value, count, collective_id):
+    shape = value.shape
+    flat = value.reshape(-1, 128)
+    summed = pl.pallas_call(
+        lambda *refs: narrow_sum_kernel(count, *refs),
+        out_shape=jax.ShapeDtypeStruct(flat.shape, flat.dtype),
+        in_specs=[pl.BlockSpec(memory_space=pltpu.VMEM)],
+        out_specs=pl.BlockSpec(memory_space=pltpu.VMEM),
+        scratch_shapes=[
+            pltpu.VMEM((count,) + flat.shape, flat.dtype),
+            pltpu.SemaphoreType.DMA((count,)),
+            pltpu.SemaphoreType.DMA((count,)),
+        ],
+        compiler_params=pltpu.CompilerParams(collective_id=collective_id, has_side_effects=True),
+    )(flat)
+    return summed.reshape(shape)
 
 
 def per_device(
@@ -36,8 +110,9 @@
     weights = (acceptor_projection, lookup_projection, payload_projection, gating_projection)
 
     floats = sublevel_symbol_entries.astype(jnp.float32)
-    stats = lax.psum(
-        jnp.stack([jnp.sum(floats, -1), jnp.sum(floats * floats, -1)], 0), "narrow"
+    count = lax.axis_size("narrow")
+    stats = narrow_sum(
+        jnp.stack([jnp.sum(floats, -1), jnp.sum(floats * floats, -1)], 0), count, 0
     )
     center = stats[0][..., None] / FEATURE_EXTENT
     spread = stats[1][..., None] / FEATURE_EXTENT - center * center
@@ -53,7 +128,7 @@
         "smd,dr->smr", blended, blending_lowering_coefficients,
         preferred_element_type=jnp.float32,
     )
-    hidden_activation = jnp.tanh(lax.psum(partial_mix, "narrow")).astype(jnp.bfloat16)
+    hidden_activation = jnp.tanh(narrow_sum(partial_mix, count, 1)).astype(jnp.bfloat16)
     decay_shift = jnp.einsum(
         "smr,rd->smd", hidden_activation[..., :rank], blending_raising_coefficients[0],
         preferred_element_type=jnp.float32,
@@ -65,7 +140,7 @@
         "smd,dr->smr", decay_mix, fading_lowering_coefficients,
         preferred_element_type=jnp.float32,
     )
-    decay_hidden = jnp.tanh(lax.psum(partial_decay, "narrow")).astype(jnp.bfloat16)
+    decay_hidden = jnp.tanh(narrow_sum(partial_decay, count, 2)).astype(jnp.bfloat16)
     small = jnp.concatenate([hidden_activation[..., rank:], decay_hidden], -1)
     small_width = small.shape[-1]
 

time: 374 us -> 345 us (0.922)
  blocking collectives: 89.4 us -> 27.7 us
  Pallas kernels: 0 us -> 25.5 us
    psum x3 -> x0, blocking collectives: 62.4 us -> none  [the longest x1 23.9 us: per_device(): lax.psum(partial_mix, 'narrow')]
    pallas_call x0 -> x3, Pallas kernels: none -> 25.5 us  [narrow_sum(): pl.pallas_call(lambda *refs: narrow_sum_kernel(count, *refs), out_shape=j...]
where the time goes in v4:
time: 345 us; the launch traced here: 344 us
  waiting for transfers between devices  208 us (60%)
  matrix products  44.3 us (13%)
  blocking collectives  27.7 us (8%)
  Pallas kernels  25.5 us (7%)
  between operations  14.3 us (4%)
  other arithmetic  12 us (3%)
  local copies, waits for them, and re-layouts  11.8 us (3%)
    all_gather x1, waiting for transfers between devices, per_device(): lax.all_gather(lax.all_gather(packed, 'x', axis=0, tiled=True), 'z', axis...  92.8 us
    all_gather x1, waiting for transfers between devices, per_device(): lax.all_gather(lax.all_gather(gated, 'x', axis=0, tiled=True), 'z', axis=...  77.6 us
    dot_general x16, matrix products, per_device(): jnp.dot(mixed_input, weights[selector_index], preferred_element_type=jnp....  38.8 us
    unnamed x4, waiting for transfers between devices  37.5 us
    pallas_call x3, Pallas kernels, narrow_sum(): pl.pallas_call(lambda *refs: narrow_sum_kernel(count, *refs), out_shape=j...  25.5 us
    all_gather x1, blocking collectives, per_device(): lax.all_gather(packed, 'x', axis=0, tiled=True)  14.7 us
    all_gather x1, blocking collectives, per_device(): lax.all_gather(gated, 'x', axis=0, tiled=True)  13 us
  transfers between devices with their start and end apart: 3, of which 3 were waited for; matrix products, arithmetic and copies ran while one was open for 0% of the time, Pallas kernels for 0%

profile of v4, /device:TPU:6, one launch (start us, length us, event | category | flops | bytes accessed | tf_op | source)
XLA Modules:
  0.0 343.9 jit_solution(3267848275260232497)
XLA Ops:
  7.2 1.0 convert_reduce_fusion
  8.3 0.1 copy.55
  8.4 0.6 reshape.712.refs_0_
  9.0 8.1 %shard_map.194 = f32[1,128]{1,0:T(1,128)} custom-call(f32[1,128]{1,0:T(1,128)} %reshape.712.refs_0_), custom_call_target="tpu_custom_call" | custom-call | tf_op jit(solution)/shard_map/pallas_call | solution.py:69
  17.1 0.8 multiply_reduce_fusion.5
  17.9 0.1 div.52
  18.0 0.1 copy.56
  18.1 0.1 div.54
  18.2 0.1 copy.57
  18.3 1.0 fusion.283
  19.3 1.0 fusion.186
  20.3 1.1 fusion.180
  21.4 0.7 reshape.713.refs_0_
  22.2 9.5 %shard_map.195 = f32[80,128]{1,0:T(8,128)} custom-call(f32[80,128]{1,0:T(8,128)} %reshape.713.refs_0_), custom_call_target="tpu_custom_call" | custom-call | tf_op jit(solution)/shard_map/pallas_call | solution.py:69
  31.7 0.8 tanh_convert_fusion
  32.5 0.1 convert_element_type.170
  32.6 0.1 slice.286
  32.7 0.7 constant_dynamic-update-slice_fusion.5
  33.4 1.1 fusion.98
  34.6 0.7 reshape.714.refs_0_
  35.3 7.9 %shard_map.196 = f32[32,128]{1,0:T(8,128)} custom-call(f32[32,128]{1,0:T(8,128)} %reshape.714.refs_0_), custom_call_target="tpu_custom_call" | custom-call | tf_op jit(solution)/shard_map/pallas_call | solution.py:69
  43.1 0.7 tanh_convert_fusion.1
  43.9 0.1 convert_element_type.173
  44.0 0.1 reshape.715
  44.1 14.7 %all_gather.12 = bf16[64,3328]{1,0:T(8,128)(2,1)} all-gather(bf16[16,3328]{1,0:T(8,128)(2,1)S(1)} %constant_dynamic-update-slice_fusion), channel_id=1, replica_groups=mesh['z'=16,'x'=4,'narrow'=8] {'x'}, dimensions={0}, use_global_device_ids=true | all-gather | bytes 532480 | tf_op jit(solution)/shard_map/all_gather | solution.py:154
  58.9 92.8 %all-gather.3.cloned.1.call-done = bf16[1024,3328]{1,0:T(8,128)(2,1)} async-done(((bf16[64,3328]{1,0:T(8,128)(2,1)}), bf16[1024,3328]{1,0:T(8,128)(2,1)}) %all-gather.3.cloned.1.call-update) | async-done | bytes 6815760 | tf_op jit(solution)/shard_map/all_gather | solution.py:153
  151.7 2.4 fusion.69
  154.1 2.5 fusion.71
  156.6 2.5 fusion.73
  159.1 2.4 fusion.75
  161.6 2.5 fusion.77
  164.0 2.4 fusion.79
  166.5 2.4 fusion.81
  168.9 2.4 fusion.83
  171.3 2.4 fusion.85
  173.7 2.4 fusion.87
  176.1 2.4 fusion.89
  178.6 2.5 fusion.91
  181.0 2.4 fusion.61
  183.5 2.4 fusion.63
  185.9 2.4 fusion.65
  188.3 2.4 fusion.67
  190.8 2.6 copy.69
  193.4 0.2 all-gather.5.cloned.1.call-start
  193.6 0.4 copy-done.2
  194.1 0.7 slice-done
  194.8 0.2 copy.61
  195.0 0.2 fusion.94
  195.2 37.5 %reduce-scatter.4.cloned.1.call-done = bf16[128,1024]{1,0:T(8,128)(2,1)} async-done(((bf16[1024,1024]{1,0:T(8,128)(2,1)}), bf16[128,1024]{1,0:T(8,128)(2,1)}) %reduce-scatter.4.cloned.1.call-update) | async-done | bytes 262160
  232.7 1.1 copy.70
  233.9 0.6 broadcast_multiply_fusion.2
  234.5 0.6 broadcast_multiply_fusion
  235.2 1.0 copy-done.1
  236.1 2.1 fusion.8
  238.2 1.9 fusion.28
  240.1 2.1 fusion.43
  242.5 0.1 fusion.205
  242.6 0.1 copy.63
  242.7 0.1 copy.64
  242.8 13.0 %all_gather.14 = bf16[256,512]{1,0:T(8,128)(2,1)} all-gather(bf16[64,512]{1,0:T(8,128)(2,1)S(1)} %copy.64), channel_id=1, replica_groups=mesh['z'=16,'x'=4,'narrow'=8] {'x'}, dimensions={0}, use_global_device_ids=true | all-gather | bytes 327680 | tf_op jit(solution)/shard_map/all_gather | solution.py:221
  255.9 77.6 %all-gather.5.cloned.1.call-done = bf16[4096,512]{1,0:T(8,128)(2,1)} async-done(((bf16[256,512]{1,0:T(8,128)(2,1)}), bf16[4096,512]{1,0:T(8,128)(2,1)}) %all-gather.5.cloned.1.call-update) | async-done | bytes 4194320 | tf_op jit(solution)/shard_map/all_gather | solution.py:220
  333.4 3.0 convolution_convert_fusion
  336.5 0.1 copy.65
  336.6 0.7 copy.66
  (59 shorter events, 0.8 us)
Async XLA Ops:
  7.2 326.3 %copy-start = (bf16[4096,64]{0,1:T(8,128)(2,1)S(1)}, bf16[4096,64]{0,1:T(8,128)(2,1)}, u32[]{:S(2)}) copy-start(bf16[4096,64]{0,1:T(8,128)(2,1)} %param.34) | copy-start | bytes 1572868
  7.2 144.5 %copy-start.5 = (bf16[5,32,512]{2,1,0:T(8,128)(2,1)S(1)}, bf16[5,32,512]{2,1,0:T(8,128)(2,1)}, u32[]{:S(2)}) copy-start(bf16[5,32,512]{2,1,0:T(8,128)(2,1)} %param.25) | copy-start | bytes 491524
  7.2 144.5 %copy-start.6 = (bf16[512,64]{0,1:T(8,128)(2,1)S(1)}, bf16[512,64]{0,1:T(8,128)(2,1)}, u32[]{:S(2)}) copy-start(bf16[512,64]{0,1:T(8,128)(2,1)} %param.30) | copy-start | bytes 196612
  7.2 144.5 %all-gather.3.cloned.1.call-start = ((), (), s32[]{:S(2)}) async-start(), calls=%async_computation.1 | async-start | bytes 7241728 | tf_op jit(solution)/shard_map/all_gather | solution.py:153
  58.8 95.3 %copy-start.7 = (bf16[512,64]{0,1:T(8,128)(2,1)S(1)}, bf16[512,64]{0,1:T(8,128)(2,1)}, u32[]{:S(2)}) copy-start(bf16[512,64]{0,1:T(8,128)(2,1)} %param.31) | copy-start | bytes 196612
  58.9 173.8 %reduce-scatter.4.cloned.1.call-start = ((), (), s32[]{:S(2)}) async-start(), calls=%async_computation.3 | async-start | bytes 2359296
  154.1 2.5 copy-start.8
  156.6 2.5 copy-start.9
  193.3 0.7 copy-start.2
  193.3 1.4 slice-start
  193.4 1.6 copy-start.10
  193.4 1.6 copy-start.11
  193.4 140.1 %all-gather.5.cloned.1.call-start = ((), (), s32[]{:S(2)}) async-start(), calls=%async_computation.2 | async-start | bytes 4456448 | tf_op jit(solution)/shard_map/all_gather | solution.py:220
  234.5 1.6 copy-start.1
  240.1 2.3 copy-start.3
  240.1 2.3 copy-start.4
Sparse Core Ops, SparseCore 0:
  59.0 92.6 all-gather.2
  193.5 39.2 reduce-scatter.3
  256.0 77.4 all-gather.4

commit v5 on v4

--- a/solution.py
+++ b/solution.py
@@ -79,6 +79,86 @@
         compiler_params=pltpu.CompilerParams(collective_id=collective_id, has_side_effects=True),
     )(flat)
     return summed.reshape(shape)
+
+
+def z_gather_kernel(size, x_ref, o_ref, buf, send_right, send_left, recv_sems):
+    me = lax.axis_index("z")
+    right = lax.rem(me + 1, size)
+    left = lax.rem(me + size - 1, size)
+
+    def device(position):
+        return (position, lax.axis_index("x"), lax.axis_index("narrow"))
+
+    barrier = pltpu.get_barrier_semaphore()
+    for neighbour in (left, right):
+        pl.semaphore_signal(
+            barrier, 1, device_id=device(neighbour), device_id_type=pl.DeviceIdType.MESH
+        )
+    pl.semaphore_wait(barrier, 2)
+
+    def send(source, origin, sem, target):
+        copy = pltpu.make_async_remote_copy(
+            src_ref=source,
+            dst_ref=buf.at[origin],
+            send_sem=sem,
+            recv_sem=recv_sems.at[origin],
+            device_id=device(target),
+            device_id_type=pl.DeviceIdType.MESH,
+        )
+        copy.start()
+        return copy
+
+    def arrived(origin):
+        pltpu.make_async_remote_copy(
+            src_ref=buf.at[origin],
+            dst_ref=buf.at[origin],
+            send_sem=send_right.at[0],
+            recv_sem=recv_sems.at[origin],
+            device_id=device(right),
+            device_id_type=pl.DeviceIdType.MESH,
+        ).wait_recv()
+
+    rightward = size // 2
+    leftward = size - 1 - rightward
+    sends = []
+    for step in range(rightward):
+        origin = lax.rem(me - step + size, size)
+        if step > 0:
+            arrived(origin)
+        source = x_ref if step == 0 else buf.at[origin]
+        sends.append(send(source, origin, send_right.at[step], right))
+        if step < leftward:
+            origin = lax.rem(me + step, size)
+            if step > 0:
+                arrived(origin)
+            source = x_ref if step == 0 else buf.at[origin]
+            sends.append(send(source, origin, send_left.at[step], left))
+    arrived(lax.rem(me - rightward + size, size))
+    if leftward > 0:
+        arrived(lax.rem(me + leftward, size))
+    for copy in sends:
+        copy.wait_send()
+    buf[me] = x_ref[...]
+    o_ref[...] = buf[...]
+
+
+def z_gather(value, size, collective_id):
+    rightward = size // 2
+    leftward = max(size - 1 - rightward, 1)
+    gathered = pl.pallas_call(
+        lambda *refs: z_gather_kernel(size, *refs),
+        out_shape=jax.ShapeDtypeStruct((size,) + value.shape, value.dtype),
+        in_specs=[pl.BlockSpec(memory_space=pltpu.VMEM)],
+        out_specs=pl.BlockSpec(memory_space=pltpu.VMEM),
+        scratch_shapes=[
+            pltpu.VMEM((size,) + value.shape, value.dtype),
+            pltpu.SemaphoreType.DMA((rightward,)),
+            pltpu.SemaphoreType.DMA((leftward,)),
+            pltpu.SemaphoreType.DMA((size,)),
+        ],
+        compiler_params=pltpu.CompilerParams(collective_id=collective_id, has_side_effects=True),
+    )(value)
+    return gathered.reshape((size * value.shape[0],) + value.shape[1:])
 
 
 def per_device(
@@ -150,9 +230,8 @@
         + [small.reshape(sessions, steps * small_width)],
         -1,
     )
-    packed_all = lax.all_gather(
-        lax.all_gather(packed, "x", axis=0, tiled=True), "z", axis=0, tiled=True
-    )
+    z_size = lax.axis_size("z")
+    packed_all = z_gather(lax.all_gather(packed, "x", axis=0, tiled=True), z_size, 3)
     small_start = (steps + 1) * features
     term_results = []
     for index in range(steps):
@@ -217,9 +296,7 @@
             ).astype(jnp.bfloat16)
         )
     gated = jnp.stack(pieces, 1).reshape(narrow_rows * steps, local_width).T
-    gated_all = lax.all_gather(
-        lax.all_gather(gated, "x", axis=0, tiled=True), "z", axis=0, tiled=True
-    )
+    gated_all = z_gather(lax.all_gather(gated, "x", axis=0, tiled=True), z_size, 4)
     mixing_output = (
         jnp.einsum(
             "cs,ce->se", gated_all, emission_projection, preferred_element_type=jnp.float32

time: 345 us -> 335 us (0.971)
  waiting for transfers between devices: 208 us -> 34.1 us
  Pallas kernels: 25.5 us -> 188 us
    all_gather x2 -> x0, waiting for transfers between devices: 170 us -> none  [the longest x1 92.8 us: per_device(): lax.all_gather(lax.all_gather(packed, 'x', axis=0, tiled=True), 'z', axis...]
    pallas_call x0 -> x2, Pallas kernels: none -> 163 us  [z_gather(): pl.pallas_call(lambda *refs: z_gather_kernel(size, *refs), out_shape=jax....]
    unnamed x4 -> x2, waiting for transfers between devices: 37.5 us -> 34.1 us
  transfers between devices with their start and end apart: 3 -> 1, of which waited for: 3 -> 1; matrix products, arithmetic and copies ran while one was open for 0% -> 1% of each run, Pallas kernels for 0% -> 0%
where the time goes in v5:
time: 335 us; the launch traced here: 333 us
  Pallas kernels  188 us (56%)
  matrix products  44.3 us (13%)
  waiting for transfers between devices  34.1 us (10%)
  blocking collectives  27.7 us (8%)
  between operations  14.6 us (4%)
  local copies, waits for them, and re-layouts  12.5 us (4%)
  other arithmetic  12 us (4%)
    pallas_call x2, Pallas kernels, z_gather(): pl.pallas_call(lambda *refs: z_gather_kernel(size, *refs), out_shape=jax....  163 us
    dot_general x16, matrix products, per_device(): jnp.dot(mixed_input, weights[selector_index], preferred_element_type=jnp....  38.8 us
    unnamed x2, waiting for transfers between devices  34.1 us
    pallas_call x3, Pallas kernels, narrow_sum(): pl.pallas_call(lambda *refs: narrow_sum_kernel(count, *refs), out_shape=j...  25.5 us
    all_gather x1, blocking collectives, per_device(): lax.all_gather(packed, 'x', axis=0, tiled=True)  14.7 us
    all_gather x1, blocking collectives, per_device(): lax.all_gather(gated, 'x', axis=0, tiled=True)  13 us
  transfers between devices with their start and end apart: 1, of which 1 were waited for; matrix products, arithmetic and copies ran while one was open for 1% of the time, Pallas kernels for 0%

profile of v5, /device:TPU:6, one launch (start us, length us, event | category | flops | bytes accessed | tf_op | source)
XLA Modules:
  0.0 333.3 jit_solution(17455976231190682181)
XLA Ops:
  7.2 1.0 convert_reduce_fusion
  8.2 0.1 copy.59
  8.3 0.6 reshape.718.refs_0_
  8.9 8.1 %shard_map.194 = f32[1,128]{1,0:T(1,128)} custom-call(f32[1,128]{1,0:T(1,128)} %reshape.718.refs_0_), custom_call_target="tpu_custom_call" | custom-call | tf_op jit(solution)/shard_map/pallas_call | solution.py:69
  17.0 0.8 multiply_reduce_fusion.5
  17.9 0.1 div.52
  18.0 0.1 copy.60
  18.0 0.1 div.54
  18.1 0.1 copy.61
  18.2 1.0 fusion.283
  19.2 1.0 fusion.186
  20.2 1.1 fusion.180
  21.4 0.7 reshape.719.refs_0_
  22.1 9.5 %shard_map.195 = f32[80,128]{1,0:T(8,128)} custom-call(f32[80,128]{1,0:T(8,128)} %reshape.719.refs_0_), custom_call_target="tpu_custom_call" | custom-call | tf_op jit(solution)/shard_map/pallas_call | solution.py:69
  31.6 0.8 tanh_convert_fusion
  32.4 0.1 convert_element_type.170
  32.5 0.1 slice.286
  32.6 0.7 constant_dynamic-update-slice_fusion.5
  33.4 1.1 fusion.98
  34.5 0.7 reshape.720.refs_0_
  35.2 7.9 %shard_map.196 = f32[32,128]{1,0:T(8,128)} custom-call(f32[32,128]{1,0:T(8,128)} %reshape.720.refs_0_), custom_call_target="tpu_custom_call" | custom-call | tf_op jit(solution)/shard_map/pallas_call | solution.py:69
  43.1 0.7 tanh_convert_fusion.1
  43.8 0.1 convert_element_type.173
  43.9 0.1 reshape.721
  44.1 14.7 %all_gather.6.refs_0_ = bf16[64,3328]{1,0:T(8,128)(2,1)} all-gather(bf16[16,3328]{1,0:T(8,128)(2,1)S(1)} %constant_dynamic-update-slice_fusion), channel_id=1, replica_groups=mesh['z'=16,'x'=4,'narrow'=8] {'x'}, dimensions={0}, use_global_device_ids=true | all-gather | bytes 532480 | tf_op jit(solution)/shard_map/all_gather | solution.py:234
  58.8 95.7 %shard_map.197 = bf16[16,64,3328]{2,1,0:T(8,128)(2,1)} custom-call(bf16[64,3328]{1,0:T(8,128)(2,1)} %all_gather.6.refs_0_), custom_call_target="tpu_custom_call" | custom-call | tf_op jit(solution)/shard_map/pallas_call | solution.py:148
  154.5 2.4 fusion.69
  156.9 2.5 fusion.71
  159.4 2.5 fusion.73
  161.9 2.4 fusion.75
  164.3 2.5 fusion.77
  166.8 2.4 fusion.79
  169.3 2.4 fusion.81
  171.6 2.4 fusion.83
  174.1 2.4 fusion.85
  176.5 2.4 fusion.87
  178.9 2.4 fusion.89
  181.4 2.5 fusion.91
  183.8 2.4 fusion.61
  186.3 2.4 fusion.63
  188.7 2.4 fusion.65
  191.1 2.4 fusion.67
  193.5 2.7 copy.73
  196.3 1.5 slice.314
  197.9 0.1 mul.757
  198.0 0.1 mul.758
  198.1 0.2 copy.65
  198.2 0.2 fusion.94
  198.5 34.1 %reduce-scatter.4.cloned.1.call-done = bf16[128,1024]{1,0:T(8,128)(2,1)} async-done(((bf16[1024,1024]{1,0:T(8,128)(2,1)}), bf16[128,1024]{1,0:T(8,128)(2,1)}) %reduce-scatter.4.cloned.1.call-update) | async-done | bytes 262160
  232.6 1.1 copy.74
  233.8 0.6 broadcast_multiply_fusion.2
  234.4 0.6 broadcast_multiply_fusion
  235.0 1.0 copy-done.1
  236.0 2.1 fusion.8
  238.1 1.9 fusion.28
  240.0 2.1 fusion.43
  242.3 0.1 fusion.205
  242.5 0.1 copy.67
  242.6 0.1 copy.68
  242.7 13.0 %all_gather.7.refs_0_ = bf16[256,512]{1,0:T(8,128)(2,1)} all-gather(bf16[64,512]{1,0:T(8,128)(2,1)S(1)} %bitcast.341), channel_id=1, replica_groups=mesh['z'=16,'x'=4,'narrow'=8] {'x'}, dimensions={0}, use_global_device_ids=true | all-gather | bytes 327680 | tf_op jit(solution)/shard_map/all_gather | solution.py:299
  255.7 66.8 %shard_map.198 = bf16[16,256,512]{2,1,0:T(8,128)(2,1)} custom-call(bf16[256,512]{1,0:T(8,128)(2,1)} %all_gather.7.refs_0_), custom_call_target="tpu_custom_call" | custom-call | tf_op jit(solution)/shard_map/pallas_call | solution.py:148
  322.6 3.0 convolution_convert_fusion
  325.6 0.1 copy.69
  325.7 0.7 copy.70
  (54 shorter events, 0.5 us)
Async XLA Ops:
  7.2 315.4 %copy-start = (bf16[4096,64]{0,1:T(8,128)(2,1)S(1)}, bf16[4096,64]{0,1:T(8,128)(2,1)}, u32[]{:S(2)}) copy-start(bf16[4096,64]{0,1:T(8,128)(2,1)} %param.34) | copy-start | bytes 1572868
  7.2 225.4 %reduce-scatter.4.cloned.1.call-start = ((), (), s32[]{:S(2)}) async-start(), calls=%async_computation.1 | async-start | bytes 2359296
  58.8 95.7 %copy-start.5 = (bf16[5,32,512]{2,1,0:T(8,128)(2,1)S(1)}, bf16[5,32,512]{2,1,0:T(8,128)(2,1)}, u32[]{:S(2)}) copy-start(bf16[5,32,512]{2,1,0:T(8,128)(2,1)} %param.25) | copy-start | bytes 491524
  58.8 95.7 %copy-start.6 = (bf16[512,64]{0,1:T(8,128)(2,1)S(1)}, bf16[512,64]{0,1:T(8,128)(2,1)}, u32[]{:S(2)}) copy-start(bf16[512,64]{0,1:T(8,128)(2,1)} %param.30) | copy-start | bytes 196612
  154.5 2.4 copy-start.7
  156.9 2.5 copy-start.8
  159.4 2.5 copy-start.9
  196.3 1.6 copy-start.2
  196.3 1.9 copy-start.10
  196.3 1.9 copy-start.11
  234.4 1.6 copy-start.1
  240.0 2.3 copy-start.3
  240.0 2.3 copy-start.4
Sparse Core Ops, SparseCore 0:
  196.4 36.1 reduce-scatter.3

commit v6 on v5

--- a/solution.py
+++ b/solution.py
@@ -159,6 +159,119 @@
         compiler_params=pltpu.CompilerParams(collective_id=collective_id, has_side_effects=True),
     )(value)
     return gathered.reshape((size * value.shape[0],) + value.shape[1:])
+
+
+def z_project_kernel(size, steps, features, x_ref, mix_ref, blend_ref, w_ref,
+                     decay_ref, terms_ref, buf, send_right, send_left, recv_sems):
+    me = lax.axis_index("z")
+    right = lax.rem(me + 1, size)
+    left = lax.rem(me + size - 1, size)
+    hidden_start = (steps + 1) * features
+    hidden_width = mix_ref.shape[1]
+    decay_start = hidden_start + steps * hidden_width
+
+    def device(position):
+        return (position, lax.axis_index("x"), lax.axis_index("narrow"))
+
+    barrier = pltpu.get_barrier_semaphore()
+    for neighbour in (left, right):
+        pl.semaphore_signal(
+            barrier, 1, device_id=device(neighbour), device_id_type=pl.DeviceIdType.MESH
+        )
+    pl.semaphore_wait(barrier, 2)
+
+    def send(source, origin, sem, target):
+        copy = pltpu.make_async_remote_copy(
+            src_ref=source,
+            dst_ref=buf.at[origin],
+            send_sem=sem,
+            recv_sem=recv_sems.at[origin],
+            device_id=device(target),
+            device_id_type=pl.DeviceIdType.MESH,
+        )
+        copy.start()
+        return copy
+
+    def arrived(origin):
+        pltpu.make_async_remote_copy(
+            src_ref=buf.at[origin],
+            dst_ref=buf.at[origin],
+            send_sem=send_right.at[0],
+            recv_sem=recv_sems.at[origin],
+            device_id=device(right),
+            device_id_type=pl.DeviceIdType.MESH,
+        ).wait_recv()
+
+    def project(block, origin):
+        selectors = w_ref.shape[0]
+        for index in range(steps):
+            previous = block[:, index * features : (index + 1) * features].astype(jnp.float32)
+            normed = block[:, (index + 1) * features : (index + 2) * features].astype(jnp.float32)
+            shifted = previous - normed
+            hidden = block[:, hidden_start + index * hidden_width : hidden_start + (index + 1) * hidden_width]
+            for selector in range(selectors):
+                low_rank = jnp.dot(hidden, mix_ref[selector], preferred_element_type=jnp.float32)
+                mixed = (
+                    normed + shifted * (blend_ref[selector + 2 : selector + 3, :] + low_rank)
+                ).astype(jnp.bfloat16)
+                terms_ref[origin, index * selectors + selector] = jnp.dot(
+                    mixed, w_ref[selector], preferred_element_type=jnp.float32
+                ).astype(terms_ref.dtype)
+
+    rightward = size // 2
+    leftward = size - 1 - rightward
+    sends = []
+    for step in range(rightward):
+        origin = lax.rem(me - step + size, size)
+        if step > 0:
+            arrived(origin)
+        source = x_ref if step == 0 else buf.at[origin]
+        sends.append(send(source, origin, send_right.at[step], right))
+        if step < leftward:
+            other = lax.rem(me + step, size)
+            if step > 0:
+                arrived(other)
+                sends.append(send(buf.at[other], other, send_left.at[step], left))
+            else:
+                sends.append(send(x_ref, other, send_left.at[step], left))
+        project(source, origin)
+        if 0 < step < leftward:
+            project(buf.at[other], other)
+    last_right = lax.rem(me - rightward + size, size)
+    arrived(last_right)
+    project(buf.at[last_right], last_right)
+    if leftward > 0:
+        last_left = lax.rem(me + leftward, size)
+        arrived(last_left)
+        project(buf.at[last_left], last_left)
+    for copy in sends:
+        copy.wait_send()
+    buf[me] = x_ref[...]
+    decay_ref[...] = buf[:, :, decay_start:]
+
+
+def z_project(value, mix, blend, stacked, size, steps, features, collective_id):
+    rightward = size // 2
+    leftward = max(size - 1 - rightward, 1)
+    rows, width = value.shape
+    selectors, _, out_width = stacked.shape
+    decay_start = (steps + 1) * features + steps * mix.shape[1]
+    return pl.pallas_call(
+        lambda *refs: z_project_kernel(size, steps, features, *refs),
+        out_shape=(
+            jax.ShapeDtypeStruct((size, rows, width - decay_start), value.dtype),
+            jax.ShapeDtypeStruct((size, steps * selectors, rows, out_width), jnp.bfloat16),
+        ),
+        in_specs=[pl.BlockSpec(memory_space=pltpu.VMEM)] * 4,
+        out_specs=(pl.BlockSpec(memory_space=pltpu.VMEM), pl.BlockSpec(memory_space=pltpu.VMEM)),
+        scratch_shapes=[
+            pltpu.VMEM((size, rows, width), value.dtype),
+            pltpu.SemaphoreType.DMA((rightward,)),
+            pltpu.SemaphoreType.DMA((leftward,)),
+            pltpu.SemaphoreType.DMA((size,)),
+        ],
+        compiler_params=pltpu.CompilerParams(collective_id=collective_id, has_side_effects=True),
+    )(value, mix, blend, stacked)
 
 
 def per_device(
@@ -221,47 +334,48 @@
         preferred_element_type=jnp.float32,
     )
     decay_hidden = jnp.tanh(narrow_sum(partial_decay, count, 2)).astype(jnp.bfloat16)
-    small = jnp.concatenate([hidden_activation[..., rank:], decay_hidden], -1)
-    small_width = small.shape[-1]
-
+    hidden_width = hidden_activation.shape[-1] - rank
+    decay_width = decay_hidden.shape[-1]
     packed = jnp.concatenate(
         [prior_symbol_memory]
         + [normed[:, index] for index in range(steps)]
-        + [small.reshape(sessions, steps * small_width)],
+        + [
+            hidden_activation[..., rank:].reshape(sessions, steps * hidden_width),
+            decay_hidden.reshape(sessions, steps * decay_width),
+        ],
         -1,
     )
+    selectors = len(weights)
+    mask = jnp.eye(selectors, dtype=blending_raising_coefficients.dtype)
+    mix_stack = jnp.einsum(
+        "ij,jrd->ijrd", mask, blending_raising_coefficients[1 : selectors + 1]
+    ).reshape(selectors, selectors * rank, features)
     z_size = lax.axis_size("z")
-    packed_all = z_gather(lax.all_gather(packed, "x", axis=0, tiled=True), z_size, 3)
-    small_start = (steps + 1) * features
-    term_results = []
-    for index in range(steps):
-        previous_now = packed_all[:, index * features : (index + 1) * features]
-        normed_now = packed_all[:, (index + 1) * features : (index + 2) * features]
-        normalized_now = normed_now.astype(jnp.float32)
-        shifted_now = previous_now.astype(jnp.float32) - normalized_now
-        small_now = small_start + index * small_width
-        for selector_index in range(4):
-            low_rank_update = jnp.dot(
-                packed_all[:, small_now + selector_index * rank : small_now + (selector_index + 1) * rank],
-                blending_raising_coefficients[selector_index + 1],
-                preferred_element_type=jnp.float32,
-            )
-            mixed_input = (
-                normalized_now
-                + shifted_now * (learned_blending[selector_index + 2] + low_rank_update)
-            ).astype(jnp.bfloat16)
-            term_results.append(
-                jnp.dot(
-                    mixed_input, weights[selector_index], preferred_element_type=jnp.float32
-                ).astype(jnp.bfloat16)
-            )
-    projected = lax.psum_scatter(
-        jnp.concatenate(term_results, -1), "narrow", scatter_dimension=0, tiled=True
-    ).astype(jnp.float32).reshape(narrow_rows, steps, 4 * local_width)
+    decay_all, terms = z_project(
+        lax.all_gather(packed, "x", axis=0, tiled=True),
+        mix_stack,
+        learned_blending,
+        jnp.stack(weights, 0),
+        z_size,
+        steps,
+        features,
+        3,
+    )
+    slots_per_device = z_size // lax.axis_size("narrow")
+    projected = lax.psum_scatter(terms, "narrow", scatter_dimension=0, tiled=True)
+    slot_rows = terms.shape[2]
+    projected = (
+        projected.reshape(slots_per_device, steps, selectors, slot_rows, local_width)
+        .transpose(0, 3, 1, 2, 4)
+        .reshape(narrow_rows, steps, selectors * local_width)
+        .astype(jnp.float32)
+    )
 
     rows_start = lax.axis_index("narrow") * narrow_rows
-    own_rows = lax.dynamic_slice_in_dim(packed_all[:, small_start:], rows_start, narrow_rows, 0)
-    decay_rows = own_rows.reshape(narrow_rows, steps, small_width)[..., 4 * rank :]
+    own_rows = lax.dynamic_slice_in_dim(
+        decay_all.reshape(-1, decay_all.shape[-1]), rows_start, narrow_rows, 0
+    )
+    decay_rows = own_rows.reshape(narrow_rows, steps, decay_width)
     decay_log = learned_fading + jnp.einsum(
         "smr,rd->smd", decay_rows, fading_raising_coefficients,
         preferred_element_type=jnp.float32,

time: 335 us -> 305 us (0.910)
  matrix products: 44.3 us -> 5.5 us
  Pallas kernels: 188 us -> 193 us
  waiting for transfers between devices: 34.1 us -> 38.6 us
    pallas_call x0 -> x1, Pallas kernels: none -> 99.8 us  [z_project(): pl.pallas_call(lambda *refs: z_project_kernel(size, steps, features, *ref...]
    pallas_call x2 -> x1, Pallas kernels: 163 us -> 67.5 us  [z_gather(): pl.pallas_call(lambda *refs: z_gather_kernel(size, *refs), out_shape=jax....]
    dot_general x16 -> x0, matrix products: 38.8 us -> none  [per_device(): jnp.dot(mixed_input, weights[selector_index], preferred_element_type=jnp....]
    reduce_scatter x0 -> x1, waiting for transfers between devices: none -> 38.6 us  [per_device(): lax.psum_scatter(terms, 'narrow', scatter_dimension=0, tiled=True)]
    unnamed x2 -> x1, waiting for transfers between devices: 34.1 us -> 0.02 us
  transfers between devices with their start and end apart: 1 -> 1, of which waited for: 1 -> 1; matrix products, arithmetic and copies ran while one was open for 1% -> 0% of each run, Pallas kernels for 0% -> 0%
where the time goes in v6:
time: 305 us; the launch traced here: 304 us
  Pallas kernels  193 us (63%)
  waiting for transfers between devices  38.6 us (13%)
  blocking collectives  27.7 us (9%)
  other arithmetic  15 us (5%)
  between operations  14.5 us (5%)
  local copies, waits for them, and re-layouts  9.8 us (3%)
  matrix products  5.5 us (2%)
    pallas_call x1, Pallas kernels, z_project(): pl.pallas_call(lambda *refs: z_project_kernel(size, steps, features, *ref...  99.8 us
    pallas_call x1, Pallas kernels, z_gather(): pl.pallas_call(lambda *refs: z_gather_kernel(size, *refs), out_shape=jax....  67.5 us
    reduce_scatter x1, waiting for transfers between devices, per_device(): lax.psum_scatter(terms, 'narrow', scatter_dimension=0, tiled=True)  38.6 us
    pallas_call x3, Pallas kernels, narrow_sum(): pl.pallas_call(lambda *refs: narrow_sum_kernel(count, *refs), out_shape=j...  25.5 us
    all_gather x1, blocking collectives, per_device(): lax.all_gather(packed, 'x', axis=0, tiled=True)  14.7 us
    all_gather x1, blocking collectives, per_device(): lax.all_gather(gated, 'x', axis=0, tiled=True)  13 us
  transfers between devices with their start and end apart: 1, of which 1 were waited for; matrix products, arithmetic and copies ran while one was open for 0% of the time, Pallas kernels for 0%

profile of v6, /device:TPU:6, one launch (start us, length us, event | category | flops | bytes accessed | tf_op | source)
XLA Modules:
  0.0 304.0 jit_solution(9827201205107511538)
XLA Ops:
  7.2 0.0 copy-start
  7.2 0.0 slice-start
  7.2 0.0 copy-start.2
  7.2 0.0 reduce-scatter.2.cloned.1.call-start
  7.3 1.1 convert_reduce_fusion
  8.3 0.8 fusion.80
  9.2 0.1 copy.36
  9.2 0.6 reshape.723.refs_0_
  9.9 8.1 %shard_map.194 = f32[1,128]{1,0:T(1,128)} custom-call(f32[1,128]{1,0:T(1,128)} %reshape.723.refs_0_), custom_call_target="tpu_custom_call" | custom-call | tf_op jit(solution)/shard_map/pallas_call | solution.py:69
  18.0 0.8 multiply_reduce_fusion.5
  18.8 0.1 div.52
  18.9 0.1 copy.37
  19.0 0.1 div.54
  19.1 0.1 copy.38
  19.1 1.0 fusion.42
  20.1 1.1 fusion.36
  21.3 0.7 reshape.724.refs_0_
  22.0 9.5 %shard_map.195 = f32[80,128]{1,0:T(8,128)} custom-call(f32[80,128]{1,0:T(8,128)} %reshape.724.refs_0_), custom_call_target="tpu_custom_call" | custom-call | tf_op jit(solution)/shard_map/pallas_call | solution.py:69
  31.6 0.8 tanh_convert_fusion
  32.4 0.1 convert_element_type.69
  32.5 0.1 slice.139
  32.6 0.7 constant_dynamic-update-slice_fusion.1
  33.3 1.1 fusion.34
  34.4 0.7 reshape.726.refs_0_
  35.1 7.9 %shard_map.196 = f32[32,128]{1,0:T(8,128)} custom-call(f32[32,128]{1,0:T(8,128)} %reshape.726.refs_0_), custom_call_target="tpu_custom_call" | custom-call | tf_op jit(solution)/shard_map/pallas_call | solution.py:69
  43.0 0.7 tanh_convert_fusion.1
  43.8 0.1 copy.41
  43.9 0.1 copy.42
  44.1 0.1 copy.43
  44.2 0.0 copy-done.5
  44.2 0.1 copy.44
  44.3 14.7 %all_gather.6.refs_0_ = bf16[64,3328]{1,0:T(8,128)(2,1)} all-gather(bf16[16,3328]{1,0:T(8,128)(2,1)S(1)} %constant_dynamic-update-slice_fusion), channel_id=1, replica_groups=mesh['z'=16,'x'=4,'narrow'=8] {'x'}, dimensions={0}, use_global_device_ids=true | all-gather | bytes 532480 | tf_op jit(solution)/shard_map/all_gather | solution.py:355
  59.1 0.9 broadcast_multiply_fusion.4
  60.0 1.0 pad_maximum_fusion.refs_3_
  60.9 99.8 %shard_map.197 = (bf16[16,64,256]{2,1,0:T(8,128)(2,1)}, bf16[16,16,64,64]{3,2,1,0:T(8,128)(2,1)}) custom-call(bf16[64,3328]{1,0:T(8,128)(2,1)} %all_gather.6.refs_0_, bf16[4,128,512]{2,1,0:T(8,128)(2,1)} %bitcast.265, f32[6,512]{1,0:T(8,128)} %refs_2_.1, bf16[4,512,64]{2,1,0:T(8,128)(2,1)} %pad_maximum_fusion.refs_3_), custom_call_target="tpu_custom_call" | custom-call | tf_op jit(solution)/shard_map/pallas_call | solution.py:259
  160.7 0.0 copy-start.7
  160.8 0.0 copy-start.6
  160.8 0.0 copy-start.8
  160.8 0.0 reduce-scatter.2.cloned.1.call-update
  160.8 0.6 copy-done.7
  161.4 0.1 mul.693
  161.5 0.1 mul.694
  161.6 0.8 constant_dynamic-slice_fusion
  162.4 0.1 copy.46
  162.5 0.2 fusion.30
  162.8 38.6 %reduce-scatter.2.cloned.1.call-done = bf16[2,16,64,64]{3,2,1,0:T(8,128)(2,1)} async-done(((bf16[16,16,64,64]{3,2,1,0:T(8,128)(2,1)}), bf16[2,16,64,64]{3,2,1,0:T(8,128)(2,1)}) %reduce-scatter.2.cloned.1.call-update) | async-done | bytes 262160 | tf_op jit(solution)/shard_map/reduce_scatter | solution.py:365
  201.4 1.1 convert_bitcast_fusion
  202.6 0.6 copy.45
  203.2 0.6 reshape.734
  203.8 0.6 broadcast_multiply_fusion.2
  204.4 0.0 copy-start.1
  204.4 0.6 broadcast_multiply_fusion
  205.0 1.0 copy-done.1
  206.0 2.1 fusion.8
  208.1 1.9 fusion.12
  210.0 2.1 fusion.27
  212.3 0.1 fusion.60
  212.5 0.1 copy.48
  212.6 0.1 copy.49
  212.7 13.0 %all_gather.7.refs_0_ = bf16[256,512]{1,0:T(8,128)(2,1)} all-gather(bf16[64,512]{1,0:T(8,128)(2,1)S(1)} %bitcast.273), channel_id=1, replica_groups=mesh['z'=16,'x'=4,'narrow'=8] {'x'}, dimensions={0}, use_global_device_ids=true | all-gather | bytes 327680 | tf_op jit(solution)/shard_map/all_gather | solution.py:413
  225.7 67.5 %shard_map.198 = bf16[16,256,512]{2,1,0:T(8,128)(2,1)} custom-call(bf16[256,512]{1,0:T(8,128)(2,1)} %all_gather.7.refs_0_), custom_call_target="tpu_custom_call" | custom-call | tf_op jit(solution)/shard_map/pallas_call | solution.py:148
  293.2 3.0 convolution_convert_fusion
  296.3 0.1 copy.50
  296.4 0.7 copy.51
  (43 shorter events, 0.4 us)
Async XLA Ops:
  7.2 286.0 %copy-start = (bf16[4096,64]{0,1:T(8,128)(2,1)S(1)}, bf16[4096,64]{0,1:T(8,128)(2,1)}, u32[]{:S(2)}) copy-start(bf16[4096,64]{0,1:T(8,128)(2,1)} %param.34) | copy-start | bytes 1572868
  7.2 51.9 %slice-start = ((bf16[5,32,512]{2,1,0:T(8,128)(2,1)}), bf16[4,32,512]{2,1,0:T(8,128)(2,1)S(1)}, s32[]{:S(2)}) async-start(bf16[5,32,512]{2,1,0:T(8,128)(2,1)} %param.25), calls=%async_computation.2 | async-start | bytes 262144 | tf_op jit(solution)/shard_map/slice | solution.py:351
  7.2 36.6 %copy-start.2 = (bf16[512,64]{0,1:T(8,128)(2,1)S(1)}, bf16[512,64]{0,1:T(8,128)(2,1)}, u32[]{:S(2)}) copy-start(bf16[512,64]{0,1:T(8,128)(2,1)} %param.30) | copy-start | bytes 196612
  7.2 36.7 %copy-start.3 = (bf16[512,64]{0,1:T(8,128)(2,1)S(1)}, bf16[512,64]{0,1:T(8,128)(2,1)}, u32[]{:S(2)}) copy-start(bf16[512,64]{0,1:T(8,128)(2,1)} %param.31) | copy-start | bytes 196612
  7.2 36.8 %copy-start.4 = (bf16[512,64]{0,1:T(8,128)(2,1)S(1)}, bf16[512,64]{0,1:T(8,128)(2,1)}, u32[]{:S(2)}) copy-start(bf16[512,64]{0,1:T(8,128)(2,1)} %param.32) | copy-start | bytes 196612
  7.2 37.0 %copy-start.5 = (bf16[512,64]{0,1:T(8,128)(2,1)S(1)}, bf16[512,64]{0,1:T(8,128)(2,1)}, u32[]{:S(2)}) copy-start(bf16[512,64]{0,1:T(8,128)(2,1)} %param.33) | copy-start | bytes 196612
  7.2 194.2 %reduce-scatter.2.cloned.1.call-start = ((), (), s32[]{:S(2)}) async-start(), calls=%async_computation.1 | async-start | bytes 4718592 | tf_op jit(solution)/shard_map/reduce_scatter | solution.py:365
  160.7 0.7 copy-start.7
  160.8 1.8 copy-start.6
  160.8 1.8 copy-start.8
  204.4 1.6 copy-start.1
  210.0 2.3 copy-start.9
  210.0 2.3 copy-start.10
Sparse Core Ops, SparseCore 0:
  160.9 40.4 reduce-scatter.1

commit v7 on v6

--- a/solution.py
+++ b/solution.py
@@ -81,20 +81,80 @@
     return summed.reshape(shape)
 
 
-def z_gather_kernel(size, x_ref, o_ref, buf, send_right, send_left, recv_sems):
+def gather_row(x_ref, buf, x_sems, local_sem, send_x, device, me, x_size):
+    mine = lax.axis_index("x")
+    rows = x_ref.shape[0]
+    local = pltpu.make_async_copy(x_ref, buf.at[me, pl.ds(mine * rows, rows)], local_sem)
+    local.start()
+    sends = []
+    for peer in range(x_size):
+        @pl.when(peer != mine)
+        def _():
+            pltpu.make_async_remote_copy(
+                src_ref=x_ref,
+                dst_ref=buf.at[me, pl.ds(mine * rows, rows)],
+                send_sem=send_x.at[peer],
+                recv_sem=x_sems.at[mine],
+                device_id=device(me, peer),
+                device_id_type=pl.DeviceIdType.MESH,
+            ).start()
+    local.wait()
+    for peer in range(x_size):
+        @pl.when(peer != mine)
+        def _():
+            pltpu.make_async_remote_copy(
+                src_ref=x_ref,
+                dst_ref=buf.at[me, pl.ds(peer * rows, rows)],
+                send_sem=send_x.at[peer],
+                recv_sem=x_sems.at[peer],
+                device_id=device(me, peer),
+                device_id_type=pl.DeviceIdType.MESH,
+            ).wait_recv()
+
+    def finish():
+        for peer in range(x_size):
+            @pl.when(peer != mine)
+            def _():
+                pltpu.make_async_remote_copy(
+                    src_ref=x_ref,
+                    dst_ref=buf.at[me, pl.ds(mine * rows, rows)],
+                    send_sem=send_x.at[peer],
+                    recv_sem=x_sems.at[mine],
+                    device_id=device(me, peer),
+                    device_id_type=pl.DeviceIdType.MESH,
+                ).wait_send()
+
+    return finish
+
+
+def greet(device, me, left, right, x_size):
+    mine = lax.axis_index("x")
+    barrier = pltpu.get_barrier_semaphore()
+    for neighbour in (left, right):
+        pl.semaphore_signal(
+            barrier, 1, device_id=device(neighbour, mine), device_id_type=pl.DeviceIdType.MESH
+        )
+    for peer in range(x_size):
+        @pl.when(peer != mine)
+        def _():
+            pl.semaphore_signal(
+                barrier, 1, device_id=device(me, peer), device_id_type=pl.DeviceIdType.MESH
+            )
+    pl.semaphore_wait(barrier, 2 + x_size - 1)
+
+
+def z_gather_kernel(size, x_size, x_ref, o_ref, buf, send_right, send_left, recv_sems,
+                    x_sems, local_sem, send_x):
     me = lax.axis_index("z")
     right = lax.rem(me + 1, size)
     left = lax.rem(me + size - 1, size)
 
-    def device(position):
-        return (position, lax.axis_index("x"), lax.axis_index("narrow"))
-
-    barrier = pltpu.get_barrier_semaphore()
-    for neighbour in (left, right):
-        pl.semaphore_signal(
-            barrier, 1, device_id=device(neighbour), device_id_type=pl.DeviceIdType.MESH
-        )
-    pl.semaphore_wait(barrier, 2)
+    def device(position, column=None):
+        column = lax.axis_index("x") if column is None else column
+        return (position, column, lax.axis_index("narrow"))
+
+    greet(device, me, left, right, x_size)
+    finish_row = gather_row(x_ref, buf, x_sems, local_sem, send_x, device, me, x_size)
 
     def send(source, origin, sem, target):
         copy = pltpu.make_async_remote_copy(
@@ -125,44 +185,49 @@
         origin = lax.rem(me - step + size, size)
         if step > 0:
             arrived(origin)
-        source = x_ref if step == 0 else buf.at[origin]
+        source = buf.at[origin]
         sends.append(send(source, origin, send_right.at[step], right))
         if step < leftward:
             origin = lax.rem(me + step, size)
             if step > 0:
                 arrived(origin)
-            source = x_ref if step == 0 else buf.at[origin]
+            source = buf.at[origin]
             sends.append(send(source, origin, send_left.at[step], left))
     arrived(lax.rem(me - rightward + size, size))
     if leftward > 0:
         arrived(lax.rem(me + leftward, size))
     for copy in sends:
         copy.wait_send()
-    buf[me] = x_ref[...]
+    finish_row()
     o_ref[...] = buf[...]
 
 
-def z_gather(value, size, collective_id):
+def z_gather(value, size, x_size, collective_id):
     rightward = size // 2
     leftward = max(size - 1 - rightward, 1)
+    row_shape = (x_size * value.shape[0],) + value.shape[1:]
     gathered = pl.pallas_call(
-        lambda *refs: z_gather_kernel(size, *refs),
-        out_shape=jax.ShapeDtypeStruct((size,) + value.shape, value.dtype),
+        lambda *refs: z_gather_kernel(size, x_size, *refs),
+        out_shape=jax.ShapeDtypeStruct((size,) + row_shape, value.dtype),
         in_specs=[pl.BlockSpec(memory_space=pltpu.VMEM)],
         out_specs=pl.BlockSpec(memory_space=pltpu.VMEM),
         scratch_shapes=[
-            pltpu.VMEM((size,) + value.shape, value.dtype),
+            pltpu.VMEM((size,) + row_shape, value.dtype),
             pltpu.SemaphoreType.DMA((rightward,)),
             pltpu.SemaphoreType.DMA((leftward,)),
             pltpu.SemaphoreType.DMA((size,)),
+            pltpu.SemaphoreType.DMA((x_size,)),
+            pltpu.SemaphoreType.DMA(()),
+            pltpu.SemaphoreType.DMA((x_size,)),
         ],
         compiler_params=pltpu.CompilerParams(collective_id=collective_id, has_side_effects=True),
     )(value)
-    return gathered.reshape((size * value.shape[0],) + value.shape[1:])
-
-
-def z_project_kernel(size, steps, features, x_ref, mix_ref, blend_ref, w_ref,
-                     decay_ref, terms_ref, buf, send_right, send_left, recv_sems):
+    return gathered.reshape((size * row_shape[0],) + value.shape[1:])
+
+
+def z_project_kernel(size, x_size, steps, features, x_ref, mix_ref, blend_ref, w_ref,
+                     decay_ref, terms_ref, buf, send_right, send_left, recv_sems,
+                     x_sems, local_sem, send_x):
     me = lax.axis_index("z")
     right = lax.rem(me + 1, size)
     left = lax.rem(me + size - 1, size)
@@ -170,15 +235,12 @@
     hidden_width = mix_ref.shape[1]
     decay_start = hidden_start + steps * hidden_width
 
-    def device(position):
-        return (position, lax.axis_index("x"), lax.axis_index("narrow"))
-
-    barrier = pltpu.get_barrier_semaphore()
-    for neighbour in (left, right):
-        pl.semaphore_signal(
-            barrier, 1, device_id=device(neighbour), device_id_type=pl.DeviceIdType.MESH
-        )
-    pl.semaphore_wait(barrier, 2)
+    def device(position, column=None):
+        column = lax.axis_index("x") if column is None else column
+        return (position, column, lax.axis_index("narrow"))
+
+    greet(device, me, left, right, x_size)
+    finish_row = gather_row(x_ref, buf, x_sems, local_sem, send_x, device, me, x_size)
 
     def send(source, origin, sem, target):
         copy = pltpu.make_async_remote_copy(
@@ -225,7 +287,7 @@
         origin = lax.rem(me - step + size, size)
         if step > 0:
             arrived(origin)
-        source = x_ref if step == 0 else buf.at[origin]
+        source = buf.at[origin]
         sends.append(send(source, origin, send_right.at[step], right))
         if step < leftward:
             other = lax.rem(me + step, size)
@@ -233,7 +295,7 @@
                 arrived(other)
                 sends.append(send(buf.at[other], other, send_left.at[step], left))
             else:
-                sends.append(send(x_ref, other, send_left.at[step], left))
+                sends.append(send(buf.at[other], other, send_left.at[step], left))
         project(source, origin)
         if 0 < step < leftward:
             project(buf.at[other], other)
@@ -246,18 +308,19 @@
         project(buf.at[last_left], last_left)
     for copy in sends:
         copy.wait_send()
-    buf[me] = x_ref[...]
+    finish_row()
     decay_ref[...] = buf[:, :, decay_start:]
 
 
-def z_project(value, mix, blend, stacked, size, steps, features, collective_id):
+def z_project(value, mix, blend, stacked, size, x_size, steps, features, collective_id):
     rightward = size // 2
     leftward = max(size - 1 - rightward, 1)
     rows, width = value.shape
+    rows = rows * x_size
     selectors, _, out_width = stacked.shape
     decay_start = (steps + 1) * features + steps * mix.shape[1]
     return pl.pallas_call(
-        lambda *refs: z_project_kernel(size, steps, features, *refs),
+        lambda *refs: z_project_kernel(size, x_size, steps, features, *refs),
         out_shape=(
             jax.ShapeDtypeStruct((size, rows, width - decay_start), value.dtype),
             jax.ShapeDtypeStruct((size, steps * selectors, rows, out_width), jnp.bfloat16),
@@ -269,6 +332,9 @@
             pltpu.SemaphoreType.DMA((rightward,)),
             pltpu.SemaphoreType.DMA((leftward,)),
             pltpu.SemaphoreType.DMA((size,)),
+            pltpu.SemaphoreType.DMA((x_size,)),
+            pltpu.SemaphoreType.DMA(()),
+            pltpu.SemaphoreType.DMA((x_size,)),
         ],
         compiler_params=pltpu.CompilerParams(collective_id=collective_id, has_side_effects=True),
     )(value, mix, blend, stacked)
@@ -351,12 +417,14 @@
         "ij,jrd->ijrd", mask, blending_raising_coefficients[1 : selectors + 1]
     ).reshape(selectors, selectors * rank, features)
     z_size = lax.axis_size("z")
+    x_size = lax.axis_size("x")
     decay_all, terms = z_project(
-        lax.all_gather(packed, "x", axis=0, tiled=True),
+        packed,
         mix_stack,
         learned_blending,
         jnp.stack(weights, 0),
         z_size,
+        x_size,
         steps,
         features,
         3,
@@ -410,7 +478,7 @@
             ).astype(jnp.bfloat16)
         )
     gated = jnp.stack(pieces, 1).reshape(narrow_rows * steps, local_width).T
-    gated_all = z_gather(lax.all_gather(gated, "x", axis=0, tiled=True), z_size, 4)
+    gated_all = z_gather(gated, z_size, x_size, 4)
     mixing_output = (
         jnp.einsum(
             "cs,ce->se", gated_all, emission_projection, preferred_element_type=jnp.float32

time: 305 us -> 286 us (0.938)
  blocking collectives: 27.7 us -> 0 us
  Pallas kernels: 193 us -> 202 us
    all_gather x2 -> x0, blocking collectives: 27.7 us -> none  [the longest x1 14.7 us: per_device(): lax.all_gather(packed, 'x', axis=0, tiled=True)]
    pallas_call x2, Pallas kernels: 167 us -> 176 us  [the longest x1 103 us: z_project(): pl.pallas_call(lambda *refs: z_project_kernel(size, x_size, steps, featur...]
where the time goes in v7:
time: 286 us; the launch traced here: 285 us
  Pallas kernels  202 us (71%)
  waiting for transfers between devices  38 us (13%)
  other arithmetic  15 us (5%)
  between operations  14.5 us (5%)
  local copies, waits for them, and re-layouts  10.4 us (4%)
  matrix products  5.5 us (2%)
    pallas_call x1, Pallas kernels, z_project(): pl.pallas_call(lambda *refs: z_project_kernel(size, x_size, steps, featur...  103 us
    pallas_call x1, Pallas kernels, z_gather(): pl.pallas_call(lambda *refs: z_gather_kernel(size, x_size, *refs), out_sh...  73 us
    reduce_scatter x1, waiting for transfers between devices, per_device(): lax.psum_scatter(terms, 'narrow', scatter_dimension=0, tiled=True)  38 us
    pallas_call x3, Pallas kernels, narrow_sum(): pl.pallas_call(lambda *refs: narrow_sum_kernel(count, *refs), out_shape=j...  25.5 us
  transfers between devices with their start and end apart: 1, of which 1 were waited for; matrix products, arithmetic and copies ran while one was open for 0% of the time, Pallas kernels for 0%

profile of v7, /device:TPU:6, one launch (start us, length us, event | category | flops | bytes accessed | tf_op | source)
XLA Modules:
  0.0 285.3 jit_solution(9152037370510386183)
XLA Ops:
  7.2 0.0 copy-start
  7.2 0.0 slice-start
  7.2 0.0 copy-start.3
  7.2 0.0 reduce-scatter.2.cloned.1.call-start
  7.3 1.1 convert_reduce_fusion
  8.3 0.8 fusion.80
  9.2 0.1 copy.36
  9.2 0.6 reshape.723.refs_0_
  9.9 8.1 %shard_map.194 = f32[1,128]{1,0:T(1,128)} custom-call(f32[1,128]{1,0:T(1,128)} %reshape.723.refs_0_), custom_call_target="tpu_custom_call" | custom-call | tf_op jit(solution)/shard_map/pallas_call | solution.py:69
  18.0 0.8 multiply_reduce_fusion.5
  18.8 0.1 div.52
  18.9 0.1 copy.37
  19.0 0.1 div.54
  19.1 0.1 copy.38
  19.1 1.0 fusion.42
  20.1 1.1 fusion.36
  21.3 0.7 reshape.724.refs_0_
  22.0 9.5 %shard_map.195 = f32[80,128]{1,0:T(8,128)} custom-call(f32[80,128]{1,0:T(8,128)} %reshape.724.refs_0_), custom_call_target="tpu_custom_call" | custom-call | tf_op jit(solution)/shard_map/pallas_call | solution.py:69
  31.6 0.8 tanh_convert_fusion
  32.4 0.1 convert_element_type.69
  32.5 0.1 slice.139
  32.6 0.7 constant_dynamic-update-slice_fusion.1
  33.3 1.1 fusion.34
  34.4 0.7 reshape.726.refs_0_
  35.1 7.9 %shard_map.196 = f32[32,128]{1,0:T(8,128)} custom-call(f32[32,128]{1,0:T(8,128)} %reshape.726.refs_0_), custom_call_target="tpu_custom_call" | custom-call | tf_op jit(solution)/shard_map/pallas_call | solution.py:69
  43.0 0.7 tanh_convert_fusion.1
  43.8 0.1 copy.41
  43.9 0.1 copy.42
  44.1 0.1 copy.43
  44.2 0.0 copy-done.6
  44.2 0.1 copy.44
  44.3 0.0 slice-done
  44.4 0.0 copy-start.2
  44.4 0.9 broadcast_multiply_fusion.4
  45.3 1.0 pad_maximum_fusion.refs_3_
  46.2 103.3 %shard_map.197 = (bf16[16,64,256]{2,1,0:T(8,128)(2,1)}, bf16[16,16,64,64]{3,2,1,0:T(8,128)(2,1)}) custom-call(bf16[16,3328]{1,0:T(8,128)(2,1)} %copy-done.2, bf16[4,128,512]{2,1,0:T(8,128)(2,1)} %bitcast.265, f32[6,512]{1,0:T(8,128)} %refs_2_.1, bf16[4,512,64]{2,1,0:T(8,128)(2,1)} %pad_maximum_fusion.refs_3_), custom_call_target="tpu_custom_call" | custom-call | tf_op jit(solution)/shard_map/pallas_call | solution.py:322
  149.6 0.0 copy-start.8
  149.6 0.0 copy-start.7
  149.6 0.0 copy-start.9
  149.6 0.0 reduce-scatter.2.cloned.1.call-update
  149.6 0.6 copy-done.8
  150.2 0.1 mul.693
  150.3 0.1 mul.694
  150.4 0.8 constant_dynamic-slice_fusion
  151.2 0.1 copy.46
  151.4 0.2 fusion.30
  151.6 38.0 %reduce-scatter.2.cloned.1.call-done = bf16[2,16,64,64]{3,2,1,0:T(8,128)(2,1)} async-done(((bf16[16,16,64,64]{3,2,1,0:T(8,128)(2,1)}), bf16[2,16,64,64]{3,2,1,0:T(8,128)(2,1)}) %reduce-scatter.2.cloned.1.call-update) | async-done | bytes 262160 | tf_op jit(solution)/shard_map/reduce_scatter | solution.py:433
  189.6 1.1 convert_bitcast_fusion
  190.7 0.6 copy.45
  191.4 0.6 reshape.734
  192.0 0.6 broadcast_multiply_fusion.2
  192.6 0.0 copy-start.1
  192.6 0.6 broadcast_multiply_fusion
  193.2 1.0 copy-done.1
  194.2 2.1 fusion.8
  196.3 1.9 fusion.12
  198.2 2.1 fusion.27
  200.5 0.1 fusion.60
  200.7 0.1 copy.48
  200.8 0.7 copy.49
  201.5 73.0 %shard_map.198 = bf16[16,256,512]{2,1,0:T(8,128)(2,1)} custom-call(bf16[64,512]{1,0:T(8,128)(2,1)} %bitcast.273), custom_call_target="tpu_custom_call" | custom-call | tf_op jit(solution)/shard_map/pallas_call | solution.py:209
  274.5 3.0 %convolution_convert_fusion = bf16[512,64]{0,1:T(8,128)(2,1)S(1)} fusion(bf16[4096,64]{0,1:T(8,128)(2,1)S(1)} %copy-done, bf16[4096,512]{1,0:T(8,128)(2,1)} %bitcast.264), kind=kOutput, calls=%fused_computation.50 | convolution fusion | flops 268468224 | bytes 4784128 | tf_op jit(solution)/shard_map/cs,ce->se/dot_general | solution.py:483
  277.6 0.1 copy.50
  277.7 0.7 copy.51
  (43 shorter events, 0.4 us)
Async XLA Ops:
  7.2 267.4 %copy-start = (bf16[4096,64]{0,1:T(8,128)(2,1)S(1)}, bf16[4096,64]{0,1:T(8,128)(2,1)}, u32[]{:S(2)}) copy-start(bf16[4096,64]{0,1:T(8,128)(2,1)} %param.34) | copy-start | bytes 1572868
  7.2 37.2 %slice-start = ((bf16[5,32,512]{2,1,0:T(8,128)(2,1)}), bf16[4,32,512]{2,1,0:T(8,128)(2,1)S(1)}, s32[]{:S(2)}) async-start(bf16[5,32,512]{2,1,0:T(8,128)(2,1)} %param.25), calls=%async_computation.2 | async-start | bytes 262144 | tf_op jit(solution)/shard_map/slice | solution.py:417
  7.2 36.6 %copy-start.3 = (bf16[512,64]{0,1:T(8,128)(2,1)S(1)}, bf16[512,64]{0,1:T(8,128)(2,1)}, u32[]{:S(2)}) copy-start(bf16[512,64]{0,1:T(8,128)(2,1)} %param.30) | copy-start | bytes 196612
  7.2 36.7 %copy-start.4 = (bf16[512,64]{0,1:T(8,128)(2,1)S(1)}, bf16[512,64]{0,1:T(8,128)(2,1)}, u32[]{:S(2)}) copy-start(bf16[512,64]{0,1:T(8,128)(2,1)} %param.31) | copy-start | bytes 196612
  7.2 36.8 %copy-start.5 = (bf16[512,64]{0,1:T(8,128)(2,1)S(1)}, bf16[512,64]{0,1:T(8,128)(2,1)}, u32[]{:S(2)}) copy-start(bf16[512,64]{0,1:T(8,128)(2,1)} %param.32) | copy-start | bytes 196612
  7.2 37.0 %copy-start.6 = (bf16[512,64]{0,1:T(8,128)(2,1)S(1)}, bf16[512,64]{0,1:T(8,128)(2,1)}, u32[]{:S(2)}) copy-start(bf16[512,64]{0,1:T(8,128)(2,1)} %param.33) | copy-start | bytes 196612
  7.2 182.3 %reduce-scatter.2.cloned.1.call-start = ((), (), s32[]{:S(2)}) async-start(), calls=%async_computation.1 | async-start | bytes 4718592 | tf_op jit(solution)/shard_map/reduce_scatter | solution.py:433
  44.4 1.9 copy-start.2
  149.6 0.7 copy-start.8
  149.6 1.8 copy-start.7
  149.6 1.8 copy-start.9
  192.6 1.6 copy-start.1
  198.2 2.3 copy-start.10
  198.2 2.3 copy-start.11
Sparse Core Ops, SparseCore 0:
  149.8 39.7 reduce-scatter.1

commit v8 on v7

--- a/solution.py
+++ b/solution.py
@@ -127,8 +127,9 @@
     return finish
 
 
-def greet(device, me, left, right, x_size):
+def greet(device, me, left, right, x_size, narrow_size=1):
     mine = lax.axis_index("x")
+    here = lax.axis_index("narrow")
     barrier = pltpu.get_barrier_semaphore()
     for neighbour in (left, right):
         pl.semaphore_signal(
@@ -140,7 +141,13 @@
             pl.semaphore_signal(
                 barrier, 1, device_id=device(me, peer), device_id_type=pl.DeviceIdType.MESH
             )
-    pl.semaphore_wait(barrier, 2 + x_size - 1)
+    for peer in range(narrow_size if narrow_size > 1 else 0):
+        @pl.when(peer != here)
+        def _():
+            pl.semaphore_signal(
+                barrier, 1, device_id=(me, mine, peer), device_id_type=pl.DeviceIdType.MESH
+            )
+    pl.semaphore_wait(barrier, 2 + x_size - 1 + (narrow_size - 1 if narrow_size > 1 else 0))
 
 
 def z_gather_kernel(size, x_size, x_ref, o_ref, buf, send_right, send_left, recv_sems,
@@ -226,8 +233,9 @@
 
 
 def z_project_kernel(size, x_size, steps, features, x_ref, mix_ref, blend_ref, w_ref,
-                     decay_ref, terms_ref, buf, send_right, send_left, recv_sems,
-                     x_sems, local_sem, send_x):
+                     decay_ref, sum_ref, buf, send_right, send_left, recv_sems,
+                     x_sems, local_sem, send_x, terms_ref, parts, part_send, part_recv,
+                     own_sems):
     me = lax.axis_index("z")
     right = lax.rem(me + 1, size)
     left = lax.rem(me + size - 1, size)
@@ -239,8 +247,31 @@
         column = lax.axis_index("x") if column is None else column
         return (position, column, lax.axis_index("narrow"))
 
-    greet(device, me, left, right, x_size)
+    narrow_size, per_owner = parts.shape[0], parts.shape[1]
+    mine = lax.axis_index("narrow")
+
+    def owner_device(owner):
+        return (me, lax.axis_index("x"), owner)
+
+    greet(device, me, left, right, x_size, narrow_size)
     finish_row = gather_row(x_ref, buf, x_sems, local_sem, send_x, device, me, x_size)
+
+    def part_copy(origin, owner):
+        return pltpu.make_async_remote_copy(
+            src_ref=terms_ref.at[origin],
+            dst_ref=parts.at[mine, lax.rem(origin, per_owner)],
+            send_sem=part_send.at[origin],
+            recv_sem=part_recv.at[mine, lax.rem(origin, per_owner)],
+            device_id=owner_device(owner),
+            device_id_type=pl.DeviceIdType.MESH,
+        )
+
+    def ship(origin):
+        owner = origin // per_owner
+
+        @pl.when(owner != mine)
+        def _():
+            part_copy(origin, owner).start()
 
     def send(source, origin, sem, target):
         copy = pltpu.make_async_remote_copy(
@@ -297,33 +328,70 @@
             else:
                 sends.append(send(buf.at[other], other, send_left.at[step], left))
         project(source, origin)
+        ship(origin)
         if 0 < step < leftward:
             project(buf.at[other], other)
+            ship(other)
     last_right = lax.rem(me - rightward + size, size)
     arrived(last_right)
     project(buf.at[last_right], last_right)
+    ship(last_right)
     if leftward > 0:
         last_left = lax.rem(me + leftward, size)
         arrived(last_left)
         project(buf.at[last_left], last_left)
+        ship(last_left)
+    own = []
+    for slot in range(per_owner):
+        copy = pltpu.make_async_copy(
+            terms_ref.at[mine * per_owner + slot], parts.at[mine, slot], own_sems.at[slot]
+        )
+        copy.start()
+        own.append(copy)
     for copy in sends:
         copy.wait_send()
     finish_row()
     decay_ref[...] = buf[:, :, decay_start:]
-
-
-def z_project(value, mix, blend, stacked, size, x_size, steps, features, collective_id):
+    for origin in range(size):
+        @pl.when(origin // per_owner != mine)
+        def _():
+            part_copy(origin, origin // per_owner).wait_send()
+    for source in range(narrow_size):
+        @pl.when(source != mine)
+        def _():
+            for slot in range(per_owner):
+                pltpu.make_async_remote_copy(
+                    src_ref=parts.at[source, slot],
+                    dst_ref=parts.at[source, slot],
+                    send_sem=part_send.at[0],
+                    recv_sem=part_recv.at[source, slot],
+                    device_id=owner_device(source),
+                    device_id_type=pl.DeviceIdType.MESH,
+                ).wait_recv()
+    for copy in own:
+        copy.wait()
+    for slot in range(per_owner):
+        total = parts[0, slot].astype(jnp.float32)
+        for source in range(1, narrow_size):
+            total = total + parts[source, slot].astype(jnp.float32)
+        sum_ref[slot] = total
+
+
+def z_project(value, mix, blend, stacked, size, x_size, narrow_size, steps, features,
+              collective_id):
     rightward = size // 2
     leftward = max(size - 1 - rightward, 1)
     rows, width = value.shape
     rows = rows * x_size
     selectors, _, out_width = stacked.shape
     decay_start = (steps + 1) * features + steps * mix.shape[1]
+    per_owner = size // narrow_size
+    term_shape = (steps * selectors, rows, out_width)
     return pl.pallas_call(
         lambda *refs: z_project_kernel(size, x_size, steps, features, *refs),
         out_shape=(
             jax.ShapeDtypeStruct((size, rows, width - decay_start), value.dtype),
-            jax.ShapeDtypeStruct((size, steps * selectors, rows, out_width), jnp.bfloat16),
+            jax.ShapeDtypeStruct((per_owner,) + term_shape, jnp.float32),
         ),
         in_specs=[pl.BlockSpec(memory_space=pltpu.VMEM)] * 4,
         out_specs=(pl.BlockSpec(memory_space=pltpu.VMEM), pl.BlockSpec(memory_space=pltpu.VMEM)),
@@ -335,6 +403,11 @@
             pltpu.SemaphoreType.DMA((x_size,)),
             pltpu.SemaphoreType.DMA(()),
             pltpu.SemaphoreType.DMA((x_size,)),
+            pltpu.VMEM((size,) + term_shape, jnp.bfloat16),
+            pltpu.VMEM((narrow_size, per_owner) + term_shape, jnp.bfloat16),
+            pltpu.SemaphoreType.DMA((size,)),
+            pltpu.SemaphoreType.DMA((narrow_size, per_owner)),
+            pltpu.SemaphoreType.DMA((per_owner,)),
         ],
         compiler_params=pltpu.CompilerParams(collective_id=collective_id, has_side_effects=True),
     )(value, mix, blend, stacked)
@@ -418,25 +491,25 @@
     ).reshape(selectors, selectors * rank, features)
     z_size = lax.axis_size("z")
     x_size = lax.axis_size("x")
-    decay_all, terms = z_project(
+    narrow_size = lax.axis_size("narrow")
+    decay_all, summed = z_project(
         packed,
         mix_stack,
         learned_blending,
         jnp.stack(weights, 0),
         z_size,
         x_size,
+        narrow_size,
         steps,
         features,
         3,
     )
-    slots_per_device = z_size // lax.axis_size("narrow")
-    projected = lax.psum_scatter(terms, "narrow", scatter_dimension=0, tiled=True)
-    slot_rows = terms.shape[2]
+    per_owner = z_size // narrow_size
+    slot_rows = summed.shape[2]
     projected = (
-        projected.reshape(slots_per_device, steps, selectors, slot_rows, local_width)
+        summed.reshape(per_owner, steps, selectors, slot_rows, local_width)
         .transpose(0, 3, 1, 2, 4)
         .reshape(narrow_rows, steps, selectors * local_width)
-        .astype(jnp.float32)
     )
 
     rows_start = lax.axis_index("narrow") * narrow_rows

time: 286 us -> 253 us (0.88)
  waiting for transfers between devices: 38 us -> 0 us
  Pallas kernels: 202 us -> 218 us
  between operations: 14.5 us -> 1.13 us
    reduce_scatter x1 -> x0, waiting for transfers between devices: 38 us -> none  [per_device(): lax.psum_scatter(terms, 'narrow', scatter_dimension=0, tiled=True)]
    pallas_call x1, Pallas kernels: 103 us -> 112 us  [z_project(): pl.pallas_call(lambda *refs: z_project_kernel(size, x_size, steps, featur...]
    pallas_call x1, Pallas kernels: 73 us -> 80.3 us  [z_gather(): pl.pallas_call(lambda *refs: z_gather_kernel(size, x_size, *refs), out_sh...]
  transfers between devices with their start and end apart: 1 -> 0, of which waited for: 1 -> 0; matrix products, arithmetic and copies ran while one was open for 0% -> 0% of each run, Pallas kernels for 0% -> 0%
where the time goes in v8:
time: 253 us; the launch traced here: 251 us
  Pallas kernels  218 us (86%)
  other arithmetic  13.8 us (5%)
  local copies, waits for them, and re-layouts  12.6 us (5%)
  matrix products  5.5 us (2%)
    pallas_call x1, Pallas kernels, z_project(): pl.pallas_call(lambda *refs: z_project_kernel(size, x_size, steps, featur...  112 us
    pallas_call x1, Pallas kernels, z_gather(): pl.pallas_call(lambda *refs: z_gather_kernel(size, x_size, *refs), out_sh...  80.3 us
    pallas_call x3, Pallas kernels, narrow_sum(): pl.pallas_call(lambda *refs: narrow_sum_kernel(count, *refs), out_shape=j...  25.5 us

profile of v8, /device:TPU:6, one launch (start us, length us, event | category | flops | bytes accessed | tf_op | source)
XLA Modules:
  0.0 251.1 jit_solution(16418373282763957955)
XLA Ops:
  0.6 0.0 copy-start
  0.6 0.0 copy-start.6
  0.7 0.0 copy-start.5
  0.7 0.0 copy-start.4
  0.7 0.0 copy-start.3
  0.7 1.0 convert_reduce_fusion
  1.7 0.0 slice-start
  1.7 0.8 fusion.80
  2.5 0.1 copy.36
  2.6 0.6 reshape.723.refs_0_
  3.2 8.1 %shard_map.194 = f32[1,128]{1,0:T(1,128)} custom-call(f32[1,128]{1,0:T(1,128)} %reshape.723.refs_0_), custom_call_target="tpu_custom_call" | custom-call | tf_op jit(solution)/shard_map/pallas_call | solution.py:69
  11.3 0.8 multiply_reduce_fusion.5
  12.2 0.1 div.52
  12.3 0.1 copy.37
  12.3 0.1 div.54
  12.5 0.1 copy.38
  12.5 0.7 mul.693
  13.3 0.1 mul.694
  13.3 1.0 fusion.42
  14.3 1.1 fusion.36
  15.5 0.7 reshape.724.refs_0_
  16.2 9.5 %shard_map.195 = f32[80,128]{1,0:T(8,128)} custom-call(f32[80,128]{1,0:T(8,128)} %reshape.724.refs_0_), custom_call_target="tpu_custom_call" | custom-call | tf_op jit(solution)/shard_map/pallas_call | solution.py:69
  25.7 0.8 tanh_convert_fusion
  26.5 0.1 convert_element_type.57
  26.7 1.1 fusion.34
  27.8 0.1 slice.139
  27.9 0.7 reshape.726.refs_0_
  28.6 7.9 %shard_map.196 = f32[32,128]{1,0:T(8,128)} custom-call(f32[32,128]{1,0:T(8,128)} %reshape.726.refs_0_), custom_call_target="tpu_custom_call" | custom-call | tf_op jit(solution)/shard_map/pallas_call | solution.py:69
  36.5 0.7 tanh_convert_fusion.1
  37.2 0.7 constant_dynamic-update-slice_fusion.1
  38.0 0.1 copy.41
  38.1 0.1 copy.42
  38.3 0.0 copy-done.5
  38.3 0.1 copy.43
  38.4 0.0 copy-done.6
  38.4 0.1 copy.44
  38.5 1.0 pad_maximum_fusion.refs_3_
  39.5 0.9 broadcast_multiply_fusion.4
  40.4 112.3 %shard_map.197 = (bf16[16,64,256]{2,1,0:T(8,128)(2,1)}, f32[2,16,64,64]{3,2,1,0:T(8,128)}) custom-call(bf16[16,3328]{1,0:T(8,128)(2,1)} %copy-done.2, bf16[4,128,512]{2,1,0:T(8,128)(2,1)} %bitcast.264, f32[6,512]{1,0:T(8,128)} %refs_2_.1, bf16[4,512,64]{2,1,0:T(8,128)(2,1)} %pad_maximum_fusion.refs_3_), custom_call_target="tpu_custom_call" | custom-call | tf_op jit(solution)/shard_map/pallas_call | solution.py:390
  152.7 0.0 copy-start.7
  152.7 0.0 copy-start.9
  152.7 0.0 copy-start.1
  152.7 0.0 copy-start.8
  152.8 2.4 copy.45
  155.2 1.8 reshape.729
  157.0 0.9 constant_dynamic-slice_fusion
  157.8 0.1 copy.46
  158.0 0.2 fusion.30
  158.3 0.0 copy-done.1
  158.3 0.0 copy-done.8
  158.3 2.1 fusion.8
  160.4 0.6 broadcast_multiply_fusion.2
  161.0 0.6 broadcast_multiply_fusion
  161.6 1.9 fusion.12
  163.5 2.1 fusion.27
  165.8 0.0 copy-done.10
  165.9 0.0 copy-done.11
  165.9 0.1 fusion.60
  166.0 0.1 copy.48
  166.1 0.7 copy.49
  166.9 80.3 %shard_map.198 = bf16[16,256,512]{2,1,0:T(8,128)(2,1)} custom-call(bf16[64,512]{1,0:T(8,128)(2,1)} %bitcast.272), custom_call_target="tpu_custom_call" | custom-call | tf_op jit(solution)/shard_map/pallas_call | solution.py:216
  247.2 3.0 %convolution_convert_fusion = bf16[512,64]{0,1:T(8,128)(2,1)S(1)} fusion(bf16[4096,64]{0,1:T(8,128)(2,1)S(1)} %copy-done, bf16[4096,512]{1,0:T(8,128)(2,1)} %bitcast.263), kind=kOutput, calls=%fused_computation.50 | convolution fusion | flops 268468224 | bytes 4784128 | tf_op jit(solution)/shard_map/cs,ce->se/dot_general | solution.py:556
  250.2 0.1 copy.50
  250.4 0.7 copy.51
  (39 shorter events, 0.4 us)
Async XLA Ops:
  0.6 246.6 %copy-start = (bf16[4096,64]{0,1:T(8,128)(2,1)S(1)}, bf16[4096,64]{0,1:T(8,128)(2,1)}, u32[]{:S(2)}) copy-start(bf16[4096,64]{0,1:T(8,128)(2,1)} %param.34) | copy-start | bytes 1572868
  0.6 37.7 %copy-start.6 = (bf16[512,64]{0,1:T(8,128)(2,1)S(1)}, bf16[512,64]{0,1:T(8,128)(2,1)}, u32[]{:S(2)}) copy-start(bf16[512,64]{0,1:T(8,128)(2,1)} %param.33) | copy-start | bytes 196612
  0.7 37.6 %copy-start.5 = (bf16[512,64]{0,1:T(8,128)(2,1)S(1)}, bf16[512,64]{0,1:T(8,128)(2,1)}, u32[]{:S(2)}) copy-start(bf16[512,64]{0,1:T(8,128)(2,1)} %param.32) | copy-start | bytes 196612
  0.7 37.5 %copy-start.4 = (bf16[512,64]{0,1:T(8,128)(2,1)S(1)}, bf16[512,64]{0,1:T(8,128)(2,1)}, u32[]{:S(2)}) copy-start(bf16[512,64]{0,1:T(8,128)(2,1)} %param.31) | copy-start | bytes 196612
  0.7 37.3 %copy-start.3 = (bf16[512,64]{0,1:T(8,128)(2,1)S(1)}, bf16[512,64]{0,1:T(8,128)(2,1)}, u32[]{:S(2)}) copy-start(bf16[512,64]{0,1:T(8,128)(2,1)} %param.30) | copy-start | bytes 196612
  1.7 37.8 %slice-start = ((bf16[5,32,512]{2,1,0:T(8,128)(2,1)}), bf16[4,32,512]{2,1,0:T(8,128)(2,1)S(1)}, s32[]{:S(2)}) async-start(bf16[5,32,512]{2,1,0:T(8,128)(2,1)} %param.25), calls=%async_computation | async-start | bytes 262144 | tf_op jit(solution)/shard_map/slice | solution.py:490
  38.0 2.4 copy-start.2
  152.7 5.3 %copy-start.7 = (bf16[64,64]{1,0:T(8,128)(2,1)S(1)}, bf16[64,64]{1,0:T(8,128)(2,1)}, u32[]{:S(2)}) copy-start(bf16[64,64]{1,0:T(8,128)(2,1)} %param.27) | copy-start | bytes 24580
  152.7 5.3 %copy-start.9 = (f32[64]{0:T(128)S(1)}, f32[64]{0:T(128)}, u32[]{:S(2)}) copy-start(f32[64]{0:T(128)} %param.28) | copy-start | bytes 772
  152.7 5.6 %copy-start.1 = (f32[4096,128]{1,0:T(8,128)S(1)}, f32[4096,128]{1,0:T(8,128)}, u32[]{:S(2)}) copy-start(f32[4096,128]{1,0:T(8,128)} %param.37) | copy-start | bytes 6291460
  152.7 5.5 %copy-start.8 = (f32[64]{0:T(128)S(1)}, f32[64]{0:T(128)}, u32[]{:S(2)}) copy-start(f32[64]{0:T(128)} %param.29) | copy-start | bytes 772
  163.5 2.3 copy-start.10
  163.5 2.3 copy-start.11

commit v9 on v8

--- a/solution.py
+++ b/solution.py
@@ -7,6 +7,7 @@
 
 CHANNEL_SPAN = 64
 FEATURE_EXTENT = 4096
+PIECES = 2
 
 
 def narrow_sum_kernel(count, x_ref, o_ref, recv, send_sems, recv_sems):
@@ -150,6 +151,64 @@
     pl.semaphore_wait(barrier, 2 + x_size - 1 + (narrow_size - 1 if narrow_size > 1 else 0))
 
 
+def run_ring(buf, me, size, left, right, device, send_right, send_left, recv_sems, on_slot):
+    pieces = recv_sems.shape[1]
+    part = buf.shape[1] // pieces
+
+    def view(origin, piece):
+        return buf.at[origin, pl.ds(piece * part, part)]
+
+    def send(origin, piece, sem, target):
+        copy = pltpu.make_async_remote_copy(
+            src_ref=view(origin, piece),
+            dst_ref=view(origin, piece),
+            send_sem=sem,
+            recv_sem=recv_sems.at[origin, piece],
+            device_id=device(target),
+            device_id_type=pl.DeviceIdType.MESH,
+        )
+        copy.start()
+        return copy
+
+    def arrived(origin, piece):
+        pltpu.make_async_remote_copy(
+            src_ref=view(origin, piece),
+            dst_ref=view(origin, piece),
+            send_sem=send_right.at[0, 0],
+            recv_sem=recv_sems.at[origin, piece],
+            device_id=device(right),
+            device_id_type=pl.DeviceIdType.MESH,
+        ).wait_recv()
+
+    rightward = size // 2
+    leftward = size - 1 - rightward
+    sends = []
+    for step in range(rightward):
+        right_origin = lax.rem(me - step + size, size)
+        left_origin = lax.rem(me + step, size) if step < leftward else None
+        for piece in range(pieces):
+            if step > 0:
+                arrived(right_origin, piece)
+            sends.append(send(right_origin, piece, send_right.at[step, piece], right))
+            if left_origin is not None:
+                if step > 0:
+                    arrived(left_origin, piece)
+                sends.append(send(left_origin, piece, send_left.at[step, piece], left))
+        on_slot(right_origin)
+        if left_origin is not None and step > 0:
+            on_slot(left_origin)
+    last_right = lax.rem(me - rightward + size, size)
+    for piece in range(pieces):
+        arrived(last_right, piece)
+    on_slot(last_right)
+    if leftward > 0:
+        last_left = lax.rem(me + leftward, size)
+        for piece in range(pieces):
+            arrived(last_left, piece)
+        on_slot(last_left)
+    return sends
+
+
 def z_gather_kernel(size, x_size, x_ref, o_ref, buf, send_right, send_left, recv_sems,
                     x_sems, local_sem, send_x):
     me = lax.axis_index("z")
@@ -163,46 +222,9 @@
     greet(device, me, left, right, x_size)
     finish_row = gather_row(x_ref, buf, x_sems, local_sem, send_x, device, me, x_size)
 
-    def send(source, origin, sem, target):
-        copy = pltpu.make_async_remote_copy(
-            src_ref=source,
-            dst_ref=buf.at[origin],
-            send_sem=sem,
-            recv_sem=recv_sems.at[origin],
-            device_id=device(target),
-            device_id_type=pl.DeviceIdType.MESH,
-        )
-        copy.start()
-        return copy
-
-    def arrived(origin):
-        pltpu.make_async_remote_copy(
-            src_ref=buf.at[origin],
-            dst_ref=buf.at[origin],
-            send_sem=send_right.at[0],
-            recv_sem=recv_sems.at[origin],
-            device_id=device(right),
-            device_id_type=pl.DeviceIdType.MESH,
-        ).wait_recv()
-
-    rightward = size // 2
-    leftward = size - 1 - rightward
-    sends = []
-    for step in range(rightward):
-        origin = lax.rem(me - step + size, size)
-        if step > 0:
-            arrived(origin)
-        source = buf.at[origin]
-        sends.append(send(source, origin, send_right.at[step], right))
-        if step < leftward:
-            origin = lax.rem(me + step, size)
-            if step > 0:
-                arrived(origin)
-            source = buf.at[origin]
-            sends.append(send(source, origin, send_left.at[step], left))
-    arrived(lax.rem(me - rightward + size, size))
-    if leftward > 0:
-        arrived(lax.rem(me + leftward, size))
+    sends = run_ring(
+        buf, me, size, left, right, device, send_right, send_left, recv_sems, lambda origin: None
+    )
     for copy in sends:
         copy.wait_send()
     finish_row()
@@ -220,9 +242,9 @@
         out_specs=pl.BlockSpec(memory_space=pltpu.VMEM),
         scratch_shapes=[
             pltpu.VMEM((size,) + row_shape, value.dtype),
-            pltpu.SemaphoreType.DMA((rightward,)),
-            pltpu.SemaphoreType.DMA((leftward,)),
-            pltpu.SemaphoreType.DMA((size,)),
+            pltpu.SemaphoreType.DMA((rightward, PIECES)),
+            pltpu.SemaphoreType.DMA((leftward, PIECES)),
+            pltpu.SemaphoreType.DMA((size, PIECES)),
             pltpu.SemaphoreType.DMA((x_size,)),
             pltpu.SemaphoreType.DMA(()),
             pltpu.SemaphoreType.DMA((x_size,)),
@@ -272,28 +294,6 @@
         @pl.when(owner != mine)
         def _():
             part_copy(origin, owner).start()
-
-    def send(source, origin, sem, target):
-        copy = pltpu.make_async_remote_copy(
-            src_ref=source,
-            dst_ref=buf.at[origin],
-            send_sem=sem,
-            recv_sem=recv_sems.at[origin],
-            device_id=device(target),
-            device_id_type=pl.DeviceIdType.MESH,
-        )
-        copy.start()
-        return copy
-
-    def arrived(origin):
-        pltpu.make_async_remote_copy(
-            src_ref=buf.at[origin],
-            dst_ref=buf.at[origin],
-            send_sem=send_right.at[0],
-            recv_sem=recv_sems.at[origin],
-            device_id=device(right),
-            device_id_type=pl.DeviceIdType.MESH,
-        ).wait_recv()
 
     def project(block, origin):
         selectors = w_ref.shape[0]
@@ -311,36 +311,13 @@
                     mixed, w_ref[selector], preferred_element_type=jnp.float32
                 ).astype(terms_ref.dtype)
 
-    rightward = size // 2
-    leftward = size - 1 - rightward
-    sends = []
-    for step in range(rightward):
-        origin = lax.rem(me - step + size, size)
-        if step > 0:
-            arrived(origin)
-        source = buf.at[origin]
-        sends.append(send(source, origin, send_right.at[step], right))
-        if step < leftward:
-            other = lax.rem(me + step, size)
-            if step > 0:
-                arrived(other)
-                sends.append(send(buf.at[other], other, send_left.at[step], left))
-            else:
-                sends.append(send(buf.at[other], other, send_left.at[step], left))
-        project(source, origin)
+    def on_slot(origin):
+        project(buf.at[origin], origin)
         ship(origin)
-        if 0 < step < leftward:
-            project(buf.at[other], other)
-            ship(other)
-    last_right = lax.rem(me - rightward + size, size)
-    arrived(last_right)
-    project(buf.at[last_right], last_right)
-    ship(last_right)
-    if leftward > 0:
-        last_left = lax.rem(me + leftward, size)
-        arrived(last_left)
-        project(buf.at[last_left], last_left)
-        ship(last_left)
+
+    sends = run_ring(
+        buf, me, size, left, right, device, send_right, send_left, recv_sems, on_slot
+    )
     own = []
     for slot in range(per_owner):
         copy = pltpu.make_async_copy(
@@ -397,9 +374,9 @@
         out_specs=(pl.BlockSpec(memory_space=pltpu.VMEM), pl.BlockSpec(memory_space=pltpu.VMEM)),
         scratch_shapes=[
             pltpu.VMEM((size, rows, width), value.dtype),
-            pltpu.SemaphoreType.DMA((rightward,)),
-            pltpu.SemaphoreType.DMA((leftward,)),
-            pltpu.SemaphoreType.DMA((size,)),
+            pltpu.SemaphoreType.DMA((rightward, PIECES)),
+            pltpu.SemaphoreType.DMA((leftward, PIECES)),
+            pltpu.SemaphoreType.DMA((size, PIECES)),
             pltpu.SemaphoreType.DMA((x_size,)),
             pltpu.SemaphoreType.DMA(()),
             pltpu.SemaphoreType.DMA((x_size,)),

time: 253 us -> 244 us (0.964)
  Pallas kernels: 218 us -> 210 us
    pallas_call x1, Pallas kernels: 80.3 us -> 73 us  [z_gather(): pl.pallas_call(lambda *refs: z_gather_kernel(size, x_size, *refs), out_sh...]
where the time goes in v9:
time: 244 us; the launch traced here: 243 us
  Pallas kernels  210 us (86%)
  other arithmetic  13.8 us (6%)
  local copies, waits for them, and re-layouts  12.6 us (5%)
  matrix products  5.5 us (2%)
    pallas_call x1, Pallas kernels, z_project(): pl.pallas_call(lambda *refs: z_project_kernel(size, x_size, steps, featur...  111 us
    pallas_call x1, Pallas kernels, z_gather(): pl.pallas_call(lambda *refs: z_gather_kernel(size, x_size, *refs), out_sh...  73 us
    pallas_call x3, Pallas kernels, narrow_sum(): pl.pallas_call(lambda *refs: narrow_sum_kernel(count, *refs), out_shape=j...  25.5 us

profile of v9, /device:TPU:6, one launch (start us, length us, event | category | flops | bytes accessed | tf_op | source)
XLA Modules:
  0.0 242.7 jit_solution(2340372217920659794)
XLA Ops:
  0.6 0.0 copy-start
  0.6 0.0 copy-start.6
  0.7 0.0 copy-start.5
  0.7 0.0 copy-start.4
  0.7 0.0 copy-start.3
  0.7 1.0 convert_reduce_fusion
  1.7 0.0 slice-start
  1.7 0.8 fusion.80
  2.5 0.1 copy.36
  2.6 0.6 reshape.723.refs_0_
  3.2 8.1 %shard_map.194 = f32[1,128]{1,0:T(1,128)} custom-call(f32[1,128]{1,0:T(1,128)} %reshape.723.refs_0_), custom_call_target="tpu_custom_call" | custom-call | tf_op jit(solution)/shard_map/pallas_call | solution.py:70
  11.3 0.8 multiply_reduce_fusion.5
  12.2 0.1 div.52
  12.3 0.1 copy.37
  12.3 0.1 div.54
  12.5 0.1 copy.38
  12.5 0.7 mul.693
  13.3 0.1 mul.694
  13.3 1.0 fusion.42
  14.3 1.1 fusion.36
  15.5 0.7 reshape.724.refs_0_
  16.2 9.5 %shard_map.195 = f32[80,128]{1,0:T(8,128)} custom-call(f32[80,128]{1,0:T(8,128)} %reshape.724.refs_0_), custom_call_target="tpu_custom_call" | custom-call | tf_op jit(solution)/shard_map/pallas_call | solution.py:70
  25.7 0.8 tanh_convert_fusion
  26.5 0.1 convert_element_type.57
  26.7 1.1 fusion.34
  27.8 0.1 slice.139
  27.9 0.7 reshape.726.refs_0_
  28.6 7.9 %shard_map.196 = f32[32,128]{1,0:T(8,128)} custom-call(f32[32,128]{1,0:T(8,128)} %reshape.726.refs_0_), custom_call_target="tpu_custom_call" | custom-call | tf_op jit(solution)/shard_map/pallas_call | solution.py:70
  36.5 0.7 tanh_convert_fusion.1
  37.2 0.7 constant_dynamic-update-slice_fusion.1
  38.0 0.0 copy-done.3
  38.0 0.0 copy-start.2
  38.0 0.1 copy.41
  38.1 0.0 copy-done.4
  38.1 0.1 copy.42
  38.3 0.0 copy-done.5
  38.3 0.1 copy.43
  38.4 0.0 copy-done.6
  38.4 0.1 copy.44
  38.5 1.0 pad_maximum_fusion.refs_3_
  39.5 0.0 slice-done
  39.5 0.9 broadcast_multiply_fusion.4
  40.4 111.2 %shard_map.197 = (bf16[16,64,256]{2,1,0:T(8,128)(2,1)}, f32[2,16,64,64]{3,2,1,0:T(8,128)}) custom-call(bf16[16,3328]{1,0:T(8,128)(2,1)} %copy-done.2, bf16[4,128,512]{2,1,0:T(8,128)(2,1)} %bitcast.264, f32[6,512]{1,0:T(8,128)} %refs_2_.1, bf16[4,512,64]{2,1,0:T(8,128)(2,1)} %pad_maximum_fusion.refs_3_), custom_call_target="tpu_custom_call" | custom-call | tf_op jit(solution)/shard_map/pallas_call | solution.py:367
  151.6 0.0 copy-start.7
  151.6 0.0 copy-start.9
  151.6 0.0 copy-start.1
  151.6 0.0 copy-start.8
  151.7 2.4 copy.45
  154.1 1.8 reshape.729
  155.9 0.9 constant_dynamic-slice_fusion
  156.7 0.1 copy.46
  156.9 0.2 fusion.30
  157.2 2.1 fusion.8
  159.3 0.6 broadcast_multiply_fusion.2
  159.9 0.6 broadcast_multiply_fusion
  160.5 1.9 fusion.12
  162.4 2.1 fusion.27
  164.8 0.1 fusion.60
  164.9 0.1 copy.48
  165.1 0.7 copy.49
  165.8 73.0 %shard_map.198 = bf16[16,256,512]{2,1,0:T(8,128)(2,1)} custom-call(bf16[64,512]{1,0:T(8,128)(2,1)} %bitcast.272), custom_call_target="tpu_custom_call" | custom-call | tf_op jit(solution)/shard_map/pallas_call | solution.py:238
  238.8 3.0 %convolution_convert_fusion = bf16[512,64]{0,1:T(8,128)(2,1)S(1)} fusion(bf16[4096,64]{0,1:T(8,128)(2,1)S(1)} %copy-done, bf16[4096,512]{1,0:T(8,128)(2,1)} %bitcast.263), kind=kOutput, calls=%fused_computation.50 | convolution fusion | flops 268468224 | bytes 4784128 | tf_op jit(solution)/shard_map/cs,ce->se/dot_general | solution.py:533
  241.8 0.1 copy.50
  242.0 0.7 copy.51
  (39 shorter events, 0.4 us)
Async XLA Ops:
  0.6 238.2 %copy-start = (bf16[4096,64]{0,1:T(8,128)(2,1)S(1)}, bf16[4096,64]{0,1:T(8,128)(2,1)}, u32[]{:S(2)}) copy-start(bf16[4096,64]{0,1:T(8,128)(2,1)} %param.34) | copy-start | bytes 1572868
  0.6 37.7 %copy-start.6 = (bf16[512,64]{0,1:T(8,128)(2,1)S(1)}, bf16[512,64]{0,1:T(8,128)(2,1)}, u32[]{:S(2)}) copy-start(bf16[512,64]{0,1:T(8,128)(2,1)} %param.33) | copy-start | bytes 196612
  0.7 37.6 %copy-start.5 = (bf16[512,64]{0,1:T(8,128)(2,1)S(1)}, bf16[512,64]{0,1:T(8,128)(2,1)}, u32[]{:S(2)}) copy-start(bf16[512,64]{0,1:T(8,128)(2,1)} %param.32) | copy-start | bytes 196612
  0.7 37.5 %copy-start.4 = (bf16[512,64]{0,1:T(8,128)(2,1)S(1)}, bf16[512,64]{0,1:T(8,128)(2,1)}, u32[]{:S(2)}) copy-start(bf16[512,64]{0,1:T(8,128)(2,1)} %param.31) | copy-start | bytes 196612
  0.7 37.3 %copy-start.3 = (bf16[512,64]{0,1:T(8,128)(2,1)S(1)}, bf16[512,64]{0,1:T(8,128)(2,1)}, u32[]{:S(2)}) copy-start(bf16[512,64]{0,1:T(8,128)(2,1)} %param.30) | copy-start | bytes 196612
  1.7 37.8 %slice-start = ((bf16[5,32,512]{2,1,0:T(8,128)(2,1)}), bf16[4,32,512]{2,1,0:T(8,128)(2,1)S(1)}, s32[]{:S(2)}) async-start(bf16[5,32,512]{2,1,0:T(8,128)(2,1)} %param.25), calls=%async_computation | async-start | bytes 262144 | tf_op jit(solution)/shard_map/slice | solution.py:467
  38.0 2.4 copy-start.2
  151.6 5.3 %copy-start.7 = (bf16[64,64]{1,0:T(8,128)(2,1)S(1)}, bf16[64,64]{1,0:T(8,128)(2,1)}, u32[]{:S(2)}) copy-start(bf16[64,64]{1,0:T(8,128)(2,1)} %param.27) | copy-start | bytes 24580
  151.6 5.3 %copy-start.9 = (f32[64]{0:T(128)S(1)}, f32[64]{0:T(128)}, u32[]{:S(2)}) copy-start(f32[64]{0:T(128)} %param.28) | copy-start | bytes 772
  151.6 5.6 %copy-start.1 = (f32[4096,128]{1,0:T(8,128)S(1)}, f32[4096,128]{1,0:T(8,128)}, u32[]{:S(2)}) copy-start(f32[4096,128]{1,0:T(8,128)} %param.37) | copy-start | bytes 6291460
  151.6 5.5 %copy-start.8 = (f32[64]{0:T(128)S(1)}, f32[64]{0:T(128)}, u32[]{:S(2)}) copy-start(f32[64]{0:T(128)} %param.29) | copy-start | bytes 772
  162.4 2.3 copy-start.10
  162.4 2.3 copy-start.11
